TPU v7x, 128 devices: a whole 4x4x4 slice. The times are simulated.
128 devices in a mesh: gx: 4 (over y), gy: 4 (over x), gz: 8 (over z, core).
Axes of the slice: x: 4, y: 4, z: 4, core: 2. Of those that a mesh axis runs over, the one named last changes fastest.
Arguments:
- hidden: bfloat16 [16384, 2, 4096], P(('gx', 'gy', 'gz')), may hold values from -6 to 6
- norm_gain: float32 [4096], replicated, may hold values from 0.25 to 1.75
- prompt_of: int32 [16384], P(('gx', 'gy', 'gz')), may hold values from 0 to 1023, as said below
- lengths: int32 [16384], P(('gx', 'gy', 'gz')), may hold values from 1 to 2
- reward_level: int32 [16384], P(('gx', 'gy', 'gz')), may hold values from 0 to 15
Outputs:
- weighted: bfloat16 [16384, 2, 4096], P(('gx', 'gy', 'gz'))
- advantages: float32 [16384], P(('gx', 'gy', 'gz'))
Inputs may be any that keep to these rules, and one draw needn't show every extreme that they name: `prompt_of`: each of the 1024 prompts has exactly 16 completions; prompt p is owned by the device p // 8 in mesh order; the completions of one device include at most 2 whose prompts one owner holds, and exactly 2 for some owner.
All inputs are finite; a program needn't handle non-finite values.
Results may differ from a plain program's by a relative error of at most 0.0085.
Values may be sent and summed in bfloat16 or wider, within the bound.
A program may use at most 64 MiB of HBM per device.

v0:
```python
import jax
import jax.numpy as jnp
from jax import lax
from jax.sharding import PartitionSpec as P

G = 16


norm_eps = 1e-05


def rms_scale(values_in, norm_gain):
    values = values_in.astype(jnp.float32)
    meansq = jnp.mean(values * values, axis=-1, keepdims=True)
    return (values * lax.rsqrt(meansq + norm_eps) * norm_gain).astype(jnp.bfloat16)


def on_device(hidden, norm_gain, prompt_of, lengths, reward_level):
    count_here, window, features = hidden.shape
    owners = lax.axis_size("gx") * lax.axis_size("gy") * lax.axis_size("gz")
    slot_count = max(2, count_here // owners + 1)
    groups = count_here // G
    owner_of = prompt_of // groups
    position = jnp.arange(count_here, dtype=jnp.int32)
    before_me = position[None, :] < position[:, None]
    same_owner = owner_of[:, None] == owner_of[None, :]
    send_slot = jnp.sum(same_owner & before_me, axis=1)
    member = prompt_of % groups
    labels = member + 1
    headers = jnp.stack([labels, reward_level, lengths], axis=1)
    slot_index = owner_of * slot_count + send_slot
    arrived = owners * slot_count
    outgoing = jnp.zeros((arrived, window, features), jnp.bfloat16).at[slot_index].set(hidden)
    header_out = jnp.zeros((arrived, 3), jnp.int32).at[slot_index].set(headers)
    incoming, header_in = (
        lax.all_to_all(outgoing, ("gx", "gy", "gz"), split_axis=0, concat_axis=0, tiled=True),
        lax.all_to_all(header_out, ("gx", "gy", "gz"), split_axis=0, concat_axis=0, tiled=True),
    )
    label_in = header_in[:, 0]
    filled = label_in > 0
    group_in = label_in - 1
    arrival = jnp.arange(arrived, dtype=jnp.int32)
    earlier_in = arrival[None, :] < arrival[:, None]
    same_group = (group_in[:, None] == group_in[None, :]) & filled[None, :]
    ranking_in = jnp.sum(same_group & earlier_in, axis=1)
    target = group_in * G + ranking_in
    target = jnp.where(filled, target, count_here)
    source = (
        jnp.zeros((count_here,), jnp.int32)
        .at[target]
        .set(jnp.arange(arrived, dtype=jnp.int32), mode="drop")
    )
    gathered = incoming[source]
    normed = rms_scale(gathered, norm_gain)
    levels = header_in[source, 1].astype(jnp.float32).reshape(groups, G)
    lengths_in = header_in[source, 2]
    average = jnp.mean(levels, axis=1, keepdims=True)
    centered = levels - average
    spread = jnp.sqrt(jnp.mean(centered * centered, axis=1, keepdims=True))
    advantages = (centered / jnp.maximum(spread, 1.0)).reshape(count_here)
    tokens_at = jnp.arange(window, dtype=jnp.int32)
    weight = jnp.where(
        tokens_at[None, :] < lengths_in[:, None],
        advantages[:, None] / lengths_in[:, None].astype(jnp.float32),
        0.0,
    )
    weighted = (normed.astype(jnp.float32) * weight[:, :, None]).astype(jnp.bfloat16)
    return (weighted, advantages)


def solution(mesh):
    in_specs = (
        P(("gx", "gy", "gz"), None, None),
        P(),
        P(("gx", "gy", "gz")),
        P(("gx", "gy", "gz")),
        P(("gx", "gy", "gz")),
    )
    out_specs = (P(("gx", "gy", "gz"), None, None), P(("gx", "gy", "gz")))
    return jax.shard_map(
        on_device, mesh=mesh, in_specs=in_specs, out_specs=out_specs, check_vma=False
    )
```

profile of v0, /device:TPU:1, one launch (start us, length us, event | category | flops | bytes accessed | tf_op | source)
XLA Modules:
  0.0 117.4 jit_solution(15211548752293268049)
XLA Ops:
  0.6 0.0 copy-start
  0.6 0.8 fusion.11
  1.5 0.2 convert_reduce_fusion.1
  1.6 0.7 pad_add_fusion
  2.3 0.1 copy.14
  2.4 1.5 %scatter_custom_fusion.1 = s32[256,3]{1,0:T(8,128)} fusion(s32[128]{0:T(128)S(1)} %compare_select_fusion.2, s32[128,3]{1,0:T(8,128)S(1)} %copy.14, s32[]{:T(128)} %constant.24.clone.1), kind=kCustom, calls=%fused_computation.22 | custom fusion | bytes 3076 | tf_op jit(solution)/shard_map/scatter | solution.py:34
  3.9 11.5 %all-to-all-start.1 = ((s32[128,2,3]{2,1,0:T(2,128)}), s32[128,2,3]{2,1,0:T(2,128)S(1)}, u32[]{:S(2)}, u32[]{:S(2)}) async-start(s32[128,2,3]{2,1,0:T(2,128)} %bitcast.3), calls=%async_computation.1 | async-start | bytes 262144 | tf_op jit(solution)/shard_map/all_to_all | solution.py:37
  15.4 6.2 %broadcast_in_dim.20 = bf16[256,2,4096]{2,1,0:T(2,128)(2,1)} broadcast(bf16[]{:T(256)} %constant.20.clone.1), dimensions={} | broadcast | bytes 4194306 | tf_op jit(solution)/shard_map/broadcast_in_dim | solution.py:33
  21.6 0.0 copy-done
  21.6 15.9 %scatter_fusion = bf16[256,2,4096]{2,1,0:T(2,128)(2,1)} fusion(bf16[256,2,4096]{2,1,0:T(2,128)(2,1)} %broadcast_in_dim.20, s32[128]{0:T(128)S(1)} %compare_select_fusion.2, bf16[128,2,4096]{2,1,0:T(2,128)(2,1)S(1)} %copy-done), kind=kCustom, calls=%fused_computation.3 | custom fusion | bytes 6291968 | tf_op jit(solution)/shard_map/scatter | solution.py:33
  37.5 0.0 all-to-all-done.1
  37.5 10.2 %all-to-all-start = ((bf16[256,2,4096]{2,1,0:T(2,128)(2,1)}), bf16[256,2,4096]{2,1,0:T(2,128)(2,1)}, u32[]{:S(2)}, u32[]{:S(2)}) async-start(bf16[256,2,4096]{2,1,0:T(2,128)(2,1)} %scatter_fusion), calls=%async_computation | async-start | bytes 8388608 | tf_op jit(solution)/shard_map/all_to_all | solution.py:36
  47.8 0.1 fusion.5
  47.9 0.0 copy-start.1
  47.9 0.1 fusion.14
  48.0 0.2 convert_reduce_fusion
  48.2 0.1 copy.15
  48.3 0.1 fusion.4
  48.5 1.6 %scatter_custom_fusion.2 = s32[128]{0:T(128)S(1)} fusion(s32[256]{0:T(256)S(1)} %fusion.4, s32[256]{0:T(256)S(1)} %iota.24, s32[]{:T(128)} %constant.24.clone.1), kind=kCustom, calls=%fused_computation.46 | custom fusion | bytes 516 | tf_op jit(solution)/shard_map/scatter | solution.py:51
  50.1 1.3 %gather_fusion.2 = s32[128]{0:T(128)S(1)} fusion(s32[256,3]{1,0:T(8,128)S(1)} %bitcast.10, s32[128]{0:T(128)S(1)} %broadcast_or_fusion.1), kind=kCustom, calls=%fused_computation.2 | custom fusion | bytes 2048 | tf_op jit(solution)/shard_map/gather | solution.py:55
  51.4 0.1 convert_element_type.45
  51.5 0.1 reduce_sum.51
  51.6 0.2 multiply_reduce_fusion
  51.8 0.1 div.53
  51.9 0.1 div.54
  51.9 0.1 sub.30
  52.0 0.1 sub.31
  52.1 1.3 %gather_fusion.1 = s32[128]{0:T(128)S(1)} fusion(s32[256,3]{1,0:T(8,128)S(1)} %bitcast.11, s32[128]{0:T(128)S(1)} %get-tuple-element.2), kind=kCustom, calls=%fused_computation.1 | custom fusion | bytes 2048 | tf_op jit(solution)/shard_map/gather | solution.py:56
  53.4 0.5 subtract_divide_fusion
  53.9 0.1 fusion.9
  54.0 46.0 %all-to-all-done = bf16[256,2,4096]{2,1,0:T(2,128)(2,1)} async-done(((bf16[256,2,4096]{2,1,0:T(2,128)(2,1)}), bf16[256,2,4096]{2,1,0:T(2,128)(2,1)}, u32[]{:S(2)}, u32[]{:S(2)}) %all-to-all-start) | async-done | bytes 4194336 | tf_op jit(solution)/shard_map/all_to_all | solution.py:36
  100.0 9.8 %gather_fusion = bf16[128,2,4096]{2,1,0:T(2,128)(2,1)S(1)} fusion(bf16[256,2,4096]{2,1,0:T(2,128)(2,1)} %all-to-all-done, s32[1024]{0:T(1024)S(1)} %pad_clamp_fusion), kind=kCustom, calls=%fused_computation | custom fusion | bytes 4194816 | tf_op jit(solution)/shard_map/gather | solution.py:53
  109.8 2.2 %fusion = f32[128,2]{1,0:T(8,128)S(1)} fusion(bf16[128,2,4096]{2,1,0:T(2,128)(2,1)S(1)} %gather_fusion), kind=kLoop, calls=%fused_computation.8 | loop fusion | flops 3145472 | bytes 2098176 | tf_op jit(solution)/shard_map/reduce_sum | solution.py:14
  112.0 0.0 copy-done.1
  112.1 5.4 %multiply_convert_fusion = bf16[128,2,4096]{2,1,0:T(2,128)(2,1)} fusion(bf16[128,2,4096]{2,1,0:T(2,128)(2,1)S(1)} %gather_fusion, f32[128,2]{1,0:T(8,128)S(1)} %fusion.9, f32[4096]{0:T(1024)S(1)} %copy-done.1, f32[128,2]{1,0:T(8,128)S(1)} %add_rsqrt_fusion), kind=kLoop, calls=%fused_computation.11 | loop fusion | flops 7340032 | bytes 4212736 | tf_op jit(solution)/shard_map/convert_element_type | solution.py:67
  (9 shorter events, 0.1 us)
Async XLA Ops:
  0.6 21.0 %copy-start = (bf16[128,2,4096]{2,1,0:T(2,128)(2,1)S(1)}, bf16[128,2,4096]{2,1,0:T(2,128)(2,1)}, u32[]{:S(2)}) copy-start(bf16[128,2,4096]{2,1,0:T(2,128)(2,1)} %param.5) | copy-start | bytes 6291460
  3.9 33.6 %all-to-all-start.1 = ((s32[128,2,3]{2,1,0:T(2,128)}), s32[128,2,3]{2,1,0:T(2,128)S(1)}, u32[]{:S(2)}, u32[]{:S(2)}) async-start(s32[128,2,3]{2,1,0:T(2,128)} %bitcast.3), calls=%async_computation.1 | async-start | bytes 262144 | tf_op jit(solution)/shard_map/all_to_all | solution.py:37
  37.5 62.4 %all-to-all-start = ((bf16[256,2,4096]{2,1,0:T(2,128)(2,1)}), bf16[256,2,4096]{2,1,0:T(2,128)(2,1)}, u32[]{:S(2)}, u32[]{:S(2)}) async-start(bf16[256,2,4096]{2,1,0:T(2,128)(2,1)} %scatter_fusion), calls=%async_computation | async-start | bytes 8388608 | tf_op jit(solution)/shard_map/all_to_all | solution.py:36
  47.9 64.2 %copy-start.1 = (f32[4096]{0:T(1024)S(1)}, f32[4096]{0:T(1024)}, u32[]{:S(2)}) copy-start(f32[4096]{0:T(1024)} %param.6) | copy-start | bytes 49156
where the time goes:
time: 118 us; the launch traced here: 117 us
  waiting for transfers between devices  46 us (39%)
  local copies, waits for them, and re-layouts  38.2 us (32%)
  starting transfers between devices  21.7 us (18%)
  other arithmetic  10.8 us (9%)
    all_to_all x1, waiting for transfers between devices, on_device(): lax.all_to_all(outgoing, ('gx', 'gy', 'gz'), split_axis=0, concat_axis=0,...  46 us
    scatter x1, local copies, waits for them, and re-layouts, on_device(): jnp.zeros((arrived, window, features), jnp.bfloat16).at[slot_index]  15.9 us
    all_to_all x1, starting transfers between devices, on_device(): lax.all_to_all(header_out, ('gx', 'gy', 'gz'), split_axis=0, concat_axis=...  11.5 us
    all_to_all x1, starting transfers between devices, on_device(): lax.all_to_all(outgoing, ('gx', 'gy', 'gz'), split_axis=0, concat_axis=0,...  10.2 us
    gather x1, local copies, waits for them, and re-layouts, on_device(): gathered = incoming[source]  9.78 us
    broadcast_in_dim x1, local copies, waits for them, and re-layouts, on_device(): jnp.zeros((arrived, window, features), jnp.bfloat16).at[slot_index]  6.22 us
    convert_element_type x1, other arithmetic, on_device(): (normed.astype(jnp.float32) * weight[:, :, None]).astype(jnp.bfloat16)  5.38 us
  transfers between devices with their start and end apart: 2, of which 1 were waited for; matrix products, arithmetic and copies ran while one was open for 24% of the time, Pallas kernels for 0%

commit v1 on v0

v1 whole, which is shorter than its diff:
```python
import functools

import jax
import jax.numpy as jnp
from jax import lax
from jax.experimental import pallas as pl
from jax.experimental.pallas import tpu as pltpu
from jax.sharding import PartitionSpec as P

MESH = pl.DeviceIdType.MESH
AXES = ("gx", "gy", "gz")
N = 128
G = 16
OWN = 8
SLOTS = 2
STRIDE = 37
norm_eps = 1e-05

NT = (((1,), (1,)), ((), ()))
NN = (((1,), (0,)), ((), ()))


def dot(a, b, dims, exact=False):
    if exact:
        return lax.dot_general(a, b, dims, precision=lax.Precision.HIGHEST,
                               preferred_element_type=jnp.float32)
    return lax.dot_general(a.astype(jnp.bfloat16), b.astype(jnp.bfloat16), dims,
                           preferred_element_type=jnp.float32)


def coords(p):
    return (p // 32, lax.rem(p // 8, 4), lax.rem(p, 8))


def shifted(me, o, sign):
    mx, my, mz, mc = me // 32, lax.rem(me // 8, 4), lax.rem(me // 2, 4), lax.rem(me, 2)
    ox, oy, oz, oc = o // 32, lax.rem(o // 8, 4), lax.rem(o // 2, 4), lax.rem(o, 2)
    x, y = lax.rem(mx + sign * ox + 4, 4), lax.rem(my + sign * oy + 4, 4)
    z, c = lax.rem(mz + sign * oz + 4, 4), lax.rem(mc + oc, 2)
    return x * 32 + y * 8 + z * 2 + c


def exchange(hidden, gain, prompt_of, lengths, reward, rows_out, table_out, adv_out,
             hbuf, gbuf, tab, itab, stab, meta, meta_in, send, recv, wtab, wsm, outv,
             in_sem, tab_sem, meta_send, meta_recv, send_sem, recv_sem, out_sem):
    me = lax.axis_index("gx") * 32 + lax.axis_index("gy") * 8 + lax.axis_index("gz")
    barrier = pltpu.get_barrier_semaphore()

    def greet(i, _):
        pl.semaphore_signal(barrier, inc=1, device_id=coords(lax.rem(me + i, N)), device_id_type=MESH)
        return 0
    lax.fori_loop(1, N, greet, 0)

    fetch_rows = pltpu.make_async_copy(hidden, hbuf, in_sem.at[0])
    fetch_gain = pltpu.make_async_copy(gain, gbuf, in_sem.at[1])
    fetch_tab = [pltpu.make_async_copy(ref, tab.at[pl.ds(k, 1)], in_sem.at[2 + k])
                 for k, ref in enumerate((prompt_of, lengths, reward))]
    for copy in fetch_tab:
        copy.start()
    fetch_rows.start()
    fetch_gain.start()
    for copy in fetch_tab:
        copy.wait()

    rows = lax.broadcasted_iota(jnp.int32, (N, N), 0)
    lanes = lax.broadcasted_iota(jnp.int32, (N, N), 1)
    before = jnp.where(rows < lanes, 1.0, 0.0)
    row8 = lax.broadcasted_iota(jnp.int32, (8, N), 0)
    lane8 = lax.broadcasted_iota(jnp.int32, (8, N), 1)

    prompt, length, level = tab[0:1], tab[1:2], tab[2:3]
    owner, label = prompt // OWN, lax.rem(prompt, OWN) + 1
    mine = owner == rows
    held = jnp.where(mine, 1.0, 0.0)
    earlier = dot(held, before, NN)
    slot0 = jnp.where(mine & (earlier < 0.5), 1.0, 0.0)
    slot1 = jnp.where(mine & (earlier == 1.0), 1.0, 0.0)
    pick = (dot(jnp.where(row8 == 0, lane8, 0).astype(jnp.float32), slot0, NT)
            + dot(jnp.where(row8 == 1, lane8, 0).astype(jnp.float32), slot1, NT))
    itab[...] = pick.astype(jnp.int32)
    to_scalar = pltpu.make_async_copy(itab, stab, tab_sem.at[0])
    to_scalar.start()
    zero = jnp.zeros((N, N), jnp.int32)
    told = jnp.where(rows == 0, label, jnp.where(rows == 1, level, jnp.where(rows == 2, length, zero)))
    told1 = jnp.where(rows == 3, label, jnp.where(rows == 4, level, jnp.where(rows == 5, length, zero)))
    meta[...] = (dot(slot0, told.astype(jnp.float32), NT) + dot(slot1, told1.astype(jnp.float32), NT)).astype(jnp.int32)
    to_scalar.wait()
    fetch_rows.wait()

    pl.semaphore_wait(barrier, N - 1)

    own_meta = pltpu.make_async_copy(meta.at[pl.ds(me, 1)], meta_in.at[pl.ds(me, 1)], meta_recv)
    own_meta.start()

    def tell(i, _):
        to = lax.rem(me + i, N)
        pltpu.make_async_remote_copy(
            src_ref=meta.at[pl.ds(to, 1)], dst_ref=meta_in.at[pl.ds(me, 1)], send_sem=meta_send, recv_sem=meta_recv,
            device_id=coords(to), device_id_type=MESH).start()
        return 0
    lax.fori_loop(1, N, tell, 0)

    def pack(i):
        to = shifted(me, lax.rem(i * STRIDE, N), 1)
        for s in range(SLOTS):
            send[to, s] = hbuf[jnp.clip(stab[s, to], 0, N - 1)]

    def ship(i):
        o = lax.rem(i * STRIDE, N)
        to = shifted(me, o, 1)
        pltpu.make_async_remote_copy(
            src_ref=send.at[to], dst_ref=recv.at[me], send_sem=send_sem, recv_sem=recv_sem.at[o],
            device_id=coords(to), device_id_type=MESH).start()

    lead = 4
    for i in range(lead):
        pack(i)

    own = pltpu.make_async_copy(send.at[me], recv.at[me], recv_sem.at[0])

    def step(i, _):
        pack(i + lead)
        ship(i)
        return 0
    pack(lead)
    own.start()
    lax.fori_loop(1, N - lead, step, 0)

    def last(i, _):
        ship(i)
        return 0
    lax.fori_loop(N - lead, N, last, 0)

    pltpu.make_async_copy(meta_in, meta_in, meta_recv).wait()
    told_in = meta_in[...].astype(jnp.float32)
    unit = jnp.where(row8 == lane8, 1.0, 0.0)
    by_source = dot(unit, told_in, NT)
    label0, label1 = by_source[0:1], by_source[3:4]
    group = (rows // G + 1).astype(jnp.float32)
    rank = lax.rem(rows, G).astype(jnp.float32)
    in0, in1 = jnp.where(label0 == group, 1.0, 0.0), jnp.where(label1 == group, 1.0, 0.0)
    ahead = dot(in0 + in1, before, NN)
    take0 = jnp.where((in0 > 0.5) & (ahead == rank), 1.0, 0.0)
    take1 = jnp.where((in1 > 0.5) & (ahead + in0 == rank), 1.0, 0.0)
    lanef = lane8.astype(jnp.float32)
    facts0 = jnp.where(row8 == 0, by_source[1:2], jnp.where(row8 == 1, by_source[2:3], jnp.where(row8 == 2, 2 * lane8, 0).astype(jnp.float32)))
    facts1 = jnp.where(row8 == 0, by_source[4:5], jnp.where(row8 == 1, by_source[5:6], jnp.where(row8 == 2, 2 * lane8 + 1, 0).astype(jnp.float32)))
    facts = dot(facts0, take0, NT) + dot(facts1, take1, NT)
    same = jnp.where(rows // G == lanes // G, 1.0, 0.0)
    mean = dot(facts, same, NN) * (1.0 / G)
    centred = facts - mean
    spread = jnp.sqrt(dot(centred * centred, same, NN, exact=True) * (1.0 / G))
    adv = centred[0:1] / jnp.maximum(spread[0:1], 1.0)
    count = facts[1:2]
    weight = adv / count
    wrows = jnp.where(row8 == 0, weight, jnp.where((row8 == 1) & (count > 1.5), weight, 0.0))
    wtab[0] = dot(wrows, take0, NN, exact=True)
    wtab[1] = dot(wrows, take1, NN, exact=True)
    weights_out = pltpu.make_async_copy(wtab, wsm, tab_sem.at[1])
    weights_out.start()
    table_out[...] = facts[2:3].astype(jnp.int32)
    adv_out[...] = adv
    weights_out.wait()
    fetch_gain.wait()

    token = lax.broadcasted_iota(jnp.int32, (2, 1), 0)
    gains = gbuf[...]

    def settle(i, _):
        o = lax.rem(i * STRIDE, N)
        src = shifted(me, o, -1)
        pltpu.make_async_copy(recv.at[src], recv.at[src], recv_sem.at[o]).wait()
        for s in range(SLOTS):
            x = recv[src, s].astype(jnp.float32)
            meansq = jnp.mean(x * x, axis=-1, keepdims=True)
            y = (x * lax.rsqrt(meansq + norm_eps) * gains).astype(jnp.bfloat16)
            w = jnp.where(token == 0, wsm[s, 0, src], wsm[s, 1, src])
            outv[src, s] = (y.astype(jnp.float32) * w).astype(jnp.bfloat16)
        return 0
    lax.fori_loop(0, N, settle, 0)
    put = pltpu.make_async_copy(outv, rows_out, out_sem)
    put.start()

    pltpu.make_async_copy(meta.at[pl.ds(0, N - 1)], meta.at[pl.ds(0, N - 1)], meta_send).wait()
    pltpu.make_async_copy(send.at[pl.ds(0, N - 1)], send.at[pl.ds(0, N - 1)], send_sem).wait()
    put.wait()


def arrange(table, adv_in, rows_in, out, adv_out, buf, in_sem, out_sem):
    CH = 16

    def load(q, _):
        pltpu.make_async_copy(rows_in.at[table[0, q]], buf.at[q], in_sem.at[q // CH]).start()
        return 0
    lax.fori_loop(0, N, load, 0)
    adv_out[...] = adv_in[...]
    for c in range(N // CH):
        part = pl.ds(c * CH, CH)
        pltpu.make_async_copy(buf.at[part], buf.at[part], in_sem.at[c]).wait()
        pltpu.make_async_copy(buf.at[part], out.at[part], out_sem).start()
    pltpu.make_async_copy(buf, buf, out_sem).wait()


def on_device(hidden, norm_gain, prompt_of, lengths, reward_level):
    count, window, features = hidden.shape
    bf16, f32, i32 = jnp.bfloat16, jnp.float32, jnp.int32
    any_space = pl.BlockSpec(memory_space=pl.ANY)
    vmem = pl.BlockSpec(memory_space=pltpu.VMEM)
    dma = pltpu.SemaphoreType.DMA
    rows, table, adv = pl.pallas_call(
        exchange,
        out_shape=(jax.ShapeDtypeStruct((N, SLOTS, window, features), bf16),
                   jax.ShapeDtypeStruct((1, N), i32), jax.ShapeDtypeStruct((1, N), f32)),
        in_specs=[any_space] * 5,
        out_specs=(any_space, vmem, vmem),
        scratch_shapes=[
            pltpu.VMEM((N, window, features), bf16), pltpu.VMEM((1, features), f32),
            pltpu.VMEM((8, N), i32), pltpu.VMEM((8, N), i32), pltpu.SMEM((8, N), i32),
            pltpu.VMEM((N, N), i32), pltpu.VMEM((N, N), i32),
            pltpu.VMEM((N, SLOTS, window, features), bf16), pltpu.VMEM((N, SLOTS, window, features), bf16),
            pltpu.VMEM((SLOTS, 8, N), f32), pltpu.SMEM((SLOTS, 8, N), f32),
            pltpu.VMEM((N, SLOTS, window, features), bf16),
            dma((5,)), dma((2,)), dma, dma, dma, dma((N,)), dma],
        compiler_params=pltpu.CompilerParams(collective_id=0, has_side_effects=True),
    )(hidden, norm_gain.reshape(1, features), prompt_of.reshape(1, N), lengths.reshape(1, N), reward_level.reshape(1, N))
    out, adv = pl.pallas_call(
        arrange,
        out_shape=(jax.ShapeDtypeStruct((N, window, features), bf16), jax.ShapeDtypeStruct((1, N), f32)),
        in_specs=[pl.BlockSpec(memory_space=pltpu.SMEM), vmem, any_space],
        out_specs=(any_space, vmem),
        scratch_shapes=[pltpu.VMEM((N, window, features), bf16), dma((8,)), dma],
    )(table, adv, rows.reshape(N * SLOTS, window, features))
    return out, adv.reshape(N)


def solution(mesh):
    spec = P(AXES)
    return jax.shard_map(
        on_device, mesh=mesh, in_specs=(P(AXES, None, None), P(), spec, spec, spec),
        out_specs=(P(AXES, None, None), spec), check_vma=False)
```

time: 118 us -> 76.6 us (0.65)
  Pallas kernels: 0 us -> 74.5 us
  waiting for transfers between devices: 46 us -> 0 us
  local copies, waits for them, and re-layouts: 38.2 us -> 0 us
  starting transfers between devices: 21.7 us -> 0 us
  other arithmetic: 10.8 us -> 0 us
    pallas_call x0 -> x2, Pallas kernels: none -> 74.5 us  [the longest x1 70.3 us: on_device(): pl.pallas_call(exchange, out_shape=(jax.ShapeDtypeStruct((N, SLOTS, windo...]
    all_to_all x2 -> x0, waiting for transfers between devices: 46 us -> none  [the longest x1 46 us: on_device(): lax.all_to_all(outgoing, ('gx', 'gy', 'gz'), split_axis=0, concat_axis=0,...]
    all_to_all x2 -> x0, starting transfers between devices: 21.7 us -> none  [the longest x1 11.5 us: on_device(): lax.all_to_all(header_out, ('gx', 'gy', 'gz'), split_axis=0, concat_axis=...]
    scatter x3 -> x0, local copies, waits for them, and re-layouts: 19 us -> none  [the longest x1 15.9 us: on_device(): jnp.zeros((arrived, window, features), jnp.bfloat16).at[slot_index]]
    gather x3 -> x0, local copies, waits for them, and re-layouts: 12.3 us -> none  [the longest x1 9.78 us: on_device(): gathered = incoming[source]]
    broadcast_in_dim x1 -> x0, local copies, waits for them, and re-layouts: 6.22 us -> none  [on_device(): jnp.zeros((arrived, window, features), jnp.bfloat16).at[slot_index]]
    convert_element_type x2 -> x0, other arithmetic: 5.38 us -> none  [the longest x1 5.38 us: on_device(): (normed.astype(jnp.float32) * weight[:, :, None]).astype(jnp.bfloat16)]
    reduce_sum x5 -> x0, other arithmetic: 2.91 us -> none  [the longest x1 2.24 us: rms_scale(): meansq = jnp.mean(values * values, axis=-1, keepdims=True)]
  transfers between devices with their start and end apart: 2 -> 0, of which waited for: 1 -> 0; matrix products, arithmetic and copies ran while one was open for 24% -> 0% of each run, Pallas kernels for 0% -> 0%
where the time goes in v1:
time: 76.6 us; the launch traced here: 75.1 us
  Pallas kernels  74.5 us (97%)
    pallas_call x1, Pallas kernels, on_device(): pl.pallas_call(exchange, out_shape=(jax.ShapeDtypeStruct((N, SLOTS, windo...  70.3 us
    pallas_call x1, Pallas kernels, on_device(): pl.pallas_call(arrange, out_shape=(jax.ShapeDtypeStruct((N, window, featu...  4.24 us

profile of v1, /device:TPU:1, one launch (start us, length us, event | category | flops | bytes accessed | tf_op | source)
XLA Modules:
  0.0 75.1 jit_solution(6834157580748305984)
XLA Ops:
  0.6 70.3 %shard_map.68 = (bf16[128,2,2,4096]{3,2,1,0:T(2,128)(2,1)}, s32[1,128]{1,0:T(1,128)}, f32[1,128]{1,0:T(1,128)}) custom-call(bf16[128,2,4096]{2,1,0:T(2,128)(2,1)} %hidden.1, f32[1,4096]{1,0:T(1,128)} %bitcast.7, s32[1,128]{1,0:T(1,128)} %bitcast.8, s32[1,128]{1,0:T(1,128)} %bitcast.9, s32[1,128]{1,0:T(1,128)} %bitcast.10), custom_call_target="tpu_custom_call" | custom-call | tf_op jit(solution)/shard_map/pallas_call | solution.py:210
  70.9 4.2 %shard_map.69 = (bf16[128,2,4096]{2,1,0:T(2,128)(2,1)}, f32[1,128]{1,0:T(1,128)}) custom-call(s32[1,128]{1,0:T(1,128)} %get-tuple-element.7.table, f32[1,128]{1,0:T(1,128)} %get-tuple-element.8.adv_in, bf16[256,2,4096]{2,1,0:T(2,128)(2,1)} %bitcast.6), custom_call_target="tpu_custom_call" | custom-call | tf_op jit(solution)/shard_map/pallas_call | solution.py:226

commit v2 on v1

v2 whole, which is shorter than its diff:
```python
import functools

import jax
import jax.numpy as jnp
from jax import lax
from jax.experimental import pallas as pl
from jax.experimental.pallas import tpu as pltpu
from jax.sharding import PartitionSpec as P

MESH = pl.DeviceIdType.MESH
AXES = ("gx", "gy", "gz")
N = 128
G = 16
OWN = 8
PIECES = 32
EARLY = 40
LATE = 120
STRIDE = 37
norm_eps = 1e-05

NT = (((1,), (1,)), ((), ()))
NN = (((1,), (0,)), ((), ()))


def dot(a, b, dims, exact=False):
    if exact:
        return lax.dot_general(a, b, dims, precision=lax.Precision.HIGHEST,
                               preferred_element_type=jnp.float32)
    return lax.dot_general(a.astype(jnp.bfloat16), b.astype(jnp.bfloat16), dims,
                           preferred_element_type=jnp.float32)


def coords(p):
    return (p // 32, lax.rem(p // 8, 4), lax.rem(p, 8))


def shifted(me, o, sign):
    mx, my, mz, mc = me // 32, lax.rem(me // 8, 4), lax.rem(me // 2, 4), lax.rem(me, 2)
    ox, oy, oz, oc = o // 32, lax.rem(o // 8, 4), lax.rem(o // 2, 4), lax.rem(o, 2)
    x, y = lax.rem(mx + sign * ox + 4, 4), lax.rem(my + sign * oy + 4, 4)
    z, c = lax.rem(mz + sign * oz + 4, 4), lax.rem(mc + oc, 2)
    return x * 32 + y * 8 + z * 2 + c


def my_place():
    return lax.axis_index("gx") * 32 + lax.axis_index("gy") * 8 + lax.axis_index("gz")


def greet_all(me):
    barrier = pltpu.get_barrier_semaphore()

    def greet(i, _):
        pl.semaphore_signal(barrier, inc=1, device_id=coords(lax.rem(me + i, N)), device_id_type=MESH)
        return 0
    lax.fori_loop(1, N, greet, 0)
    return barrier


def slots_of(owner, rows, before):
    mine = owner == rows
    earlier = dot(jnp.where(mine, 1.0, 0.0), before, NN)
    slot0 = jnp.where(mine & (earlier < 0.5), 1.0, 0.0)
    slot1 = jnp.where(mine & (earlier == 1.0), 1.0, 0.0)
    return slot0, slot1


def bounded(i, n):
    return jnp.clip(i, 0, n - 1)


def scaled(x, gains, w0, w1):
    token = lax.broadcasted_iota(jnp.int32, (2, 1), 0)
    x = x.astype(jnp.float32)
    meansq = jnp.mean(x * x, axis=-1, keepdims=True)
    y = (x * lax.rsqrt(meansq + norm_eps) * gains).astype(jnp.bfloat16)
    return (y.astype(jnp.float32) * jnp.where(token == 0, w0, w1)).astype(jnp.bfloat16)


def row_traffic(me, hbuf, stab, send, recv, send_sem, recv_sem):
    def pack(i):
        to = shifted(me, lax.rem(i * STRIDE, N), 1)
        send[to] = hbuf[bounded(stab[0, to], N)]

    def ship(i):
        o = lax.rem(i * STRIDE, N)
        to = shifted(me, o, 1)
        pltpu.make_async_remote_copy(
            src_ref=send.at[to], dst_ref=recv.at[me], send_sem=send_sem, recv_sem=recv_sem.at[o],
            device_id=coords(to), device_id_type=MESH).start()

    def await_row(i):
        o = lax.rem(i * STRIDE, N)
        src = shifted(me, o, -1)
        pltpu.make_async_copy(recv.at[src], recv.at[src], recv_sem.at[o]).wait()
        return src
    own = pltpu.make_async_copy(send.at[me], recv.at[me], recv_sem.at[0])
    return pack, ship, await_row, own


def drained(ref, sem):
    part = ref.at[pl.ds(0, N - 1)]
    pltpu.make_async_copy(part, part, sem).wait()


def exchange(hidden, gain, prompt_of, lengths, reward, rows_out, table_out, adv_out, weights_out,
             hbuf, gbuf, tab, itab, stab, jtab, ttab, meta, meta_in, extra, piece_in, part, part_in, extra_in,
             send, recv, wtab, wsm, outv,
             in_sem, tab_sem, meta_send, meta_recv, piece_send, piece_recv, part_send, part_recv,
             send_sem, recv_sem, out_sem):
    me = my_place()
    barrier = greet_all(me)

    fetch_rows = pltpu.make_async_copy(hidden, hbuf, in_sem.at[0])
    fetch_gain = pltpu.make_async_copy(gain, gbuf, in_sem.at[1])
    fetch_tab = [pltpu.make_async_copy(ref, tab.at[pl.ds(k, 1)], in_sem.at[2 + k])
                 for k, ref in enumerate((prompt_of, lengths, reward))]
    for copy in fetch_tab:
        copy.start()
    fetch_rows.start()
    fetch_gain.start()
    for copy in fetch_tab:
        copy.wait()

    rows = lax.broadcasted_iota(jnp.int32, (N, N), 0)
    lanes = lax.broadcasted_iota(jnp.int32, (N, N), 1)
    before = jnp.where(rows < lanes, 1.0, 0.0)
    row8 = lax.broadcasted_iota(jnp.int32, (8, N), 0)
    lane8 = lax.broadcasted_iota(jnp.int32, (8, N), 1)
    lane1 = lax.broadcasted_iota(jnp.int32, (1, N), 1)
    lanef = lane8.astype(jnp.float32)

    prompt, length, level = tab[0:1], tab[1:2], tab[2:3]
    owner, label = prompt // OWN, lax.rem(prompt, OWN) + 1
    slot0, slot1 = slots_of(owner, rows, before)
    twice = jnp.sum(slot1, axis=0, keepdims=True)
    spare = jnp.sum(twice, axis=1, keepdims=True)
    spare_row = jnp.sum(twice * lane1.astype(jnp.float32), axis=1, keepdims=True)
    spare_to = jnp.where(spare > 0.5, jnp.sum(twice * owner.astype(jnp.float32), axis=1, keepdims=True), -1.0)
    pick = jnp.where(row8 == 0, dot(lanef, slot0, NT), spare_row)
    itab[...] = pick.astype(jnp.int32)
    to_scalar = pltpu.make_async_copy(itab, stab, tab_sem.at[0])
    to_scalar.start()
    zero = jnp.zeros((N, N), jnp.int32)
    told = jnp.where(rows == 0, label, jnp.where(rows == 1, level, jnp.where(rows == 2, length, zero)))
    told1 = jnp.where(rows == 3, label, jnp.where(rows == 4, level, jnp.where(rows == 5, length, zero)))
    meta[...] = (dot(slot0, told.astype(jnp.float32), NT) + dot(slot1, told1.astype(jnp.float32), NT)
                 + jnp.where(lanes == 6, spare_to, jnp.where(lanes == 7, spare, 0.0))).astype(jnp.int32)
    to_scalar.wait()
    fetch_rows.wait()
    extra[...] = hbuf[bounded(stab[1, 0], N)]

    pack, ship, await_row, own = row_traffic(me, hbuf, stab, send, recv, send_sem, recv_sem)
    lead = 4
    for i in range(lead):
        pack(i)
    own_meta = pltpu.make_async_copy(meta.at[pl.ds(me, 1)], meta_in.at[pl.ds(me, 1)], meta_recv)
    own_piece = pltpu.make_async_copy(extra.at[:, pl.ds(0, 128)], piece_in.at[me // 4], piece_recv)
    own_meta.start()
    own_piece.start()

    pl.semaphore_wait(barrier, N - 1)

    def tell(i, _):
        to = lax.rem(me + i, N)
        pltpu.make_async_remote_copy(
            src_ref=meta.at[pl.ds(to, 1)], dst_ref=meta_in.at[pl.ds(me, 1)], send_sem=meta_send, recv_sem=meta_recv,
            device_id=coords(to), device_id_type=MESH).start()
        return 0

    def hand(t, _):
        to = lax.rem(me + 4 * t, N)
        pltpu.make_async_remote_copy(
            src_ref=extra.at[:, pl.ds(pl.multiple_of(t * 128, 128), 128)], dst_ref=piece_in.at[me // 4],
            send_sem=piece_send, recv_sem=piece_recv, device_id=coords(to), device_id_type=MESH).start()
        return 0
    lax.fori_loop(1, N, tell, 0)
    lax.fori_loop(1, PIECES, hand, 0)

    def step(i, _):
        pack(i + lead)
        ship(i)
        return 0
    pack(lead)
    own.start()
    lax.fori_loop(1, EARLY, step, 0)

    pltpu.make_async_copy(meta_in, meta_in, meta_recv).wait()
    told_in = meta_in[...].astype(jnp.float32)
    by_source = dot(jnp.where(row8 == lane8, 1.0, 0.0), told_in, NT)
    label0, label1, to1, spares = by_source[0:1], by_source[3:4], by_source[6:7], by_source[7:8]
    mef = me.astype(jnp.float32)

    passing = jnp.where((to1 == rows.astype(jnp.float32)) & (lax.rem(lane1, 4) == lax.rem(me, 4)), 1.0, 0.0)
    piece_of = dot((lane8 // 4).astype(jnp.float32), passing, NT)
    here = jnp.where(to1 == mef, 1.0, 0.0)
    giver = jnp.sum(here * lane1.astype(jnp.float32), axis=1, keepdims=True)
    jtab[...] = jnp.where(row8 == 0, piece_of, giver).astype(jnp.int32)
    to_scalar = pltpu.make_async_copy(jtab, ttab, tab_sem.at[0])
    to_scalar.start()

    group = (rows // G + 1).astype(jnp.float32)
    rank = lax.rem(rows, G).astype(jnp.float32)
    in0, in1 = jnp.where(label0 == group, 1.0, 0.0), jnp.where(label1 == group, 1.0, 0.0)
    ahead = dot(in0 + in1, before, NN)
    take0 = jnp.where((in0 > 0.5) & (ahead == rank), 1.0, 0.0)
    take1 = jnp.where((in1 > 0.5) & (ahead + in0 == rank), 1.0, 0.0)

    to_scalar.wait()
    pltpu.make_async_copy(piece_in, piece_in, piece_recv).wait()

    def sort_part(d, _):
        part[d] = piece_in[bounded(ttab[0, d], PIECES)]
        return 0
    lax.fori_loop(0, N, sort_part, 0)

    crowd = jnp.sum(jnp.where(to1 == rows.astype(jnp.float32), 1.0, 0.0), axis=1, keepdims=True)
    worst = jnp.maximum(jnp.max(crowd, axis=0, keepdims=True), jnp.max(spares, axis=1, keepdims=True))
    facts0 = jnp.where(row8 == 0, by_source[1:2], jnp.where(row8 == 1, by_source[2:3], lanef))
    facts1 = jnp.where(row8 == 0, by_source[4:5], jnp.where(row8 == 1, by_source[5:6], jnp.where(row8 == 2, 1.0 * N, lanef + N)))
    facts = dot(facts0, take0, NT) + dot(facts1, take1, NT)

    own_part = pltpu.make_async_copy(part.at[me], part_in.at[me], part_recv)
    own_part.start()

    def pass_on(i, _):
        to = lax.rem(me + i, N)
        pltpu.make_async_remote_copy(
            src_ref=part.at[to], dst_ref=part_in.at[me], send_sem=part_send, recv_sem=part_recv,
            device_id=coords(to), device_id_type=MESH).start()
        return 0
    lax.fori_loop(1, N, pass_on, 0)

    lax.fori_loop(EARLY, N - lead, step, 0)

    def last(i, _):
        ship(i)
        return 0
    lax.fori_loop(N - lead, N, last, 0)

    same = jnp.where(rows // G == lanes // G, 1.0, 0.0)
    mean = dot(facts, same, NN) * (1.0 / G)
    centred = facts - mean
    spread = jnp.sqrt(dot(centred * centred, same, NN, exact=True) * (1.0 / G))
    adv = centred[0:1] / jnp.maximum(spread[0:1], 1.0)
    count = facts[1:2]
    weight = adv / count
    wrows = jnp.where(row8 == 0, weight, jnp.where((row8 == 1) & (count > 1.5), weight, 0.0))
    by0, by1 = dot(wrows, take0, NN, exact=True), dot(wrows, take1, NN, exact=True)
    mine1 = jnp.sum(by1 * here, axis=1, keepdims=True)
    wtab[0] = by0
    wtab[1] = mine1 + jnp.zeros((8, N), jnp.float32)
    to_scalar = pltpu.make_async_copy(wtab, wsm, tab_sem.at[1])
    to_scalar.start()
    weights_out[...] = by1
    table_out[...] = jnp.where(row8 == 0, facts[2:3], jnp.where(row8 == 1, facts[3:4], worst)).astype(jnp.int32)
    adv_out[...] = adv
    to_scalar.wait()
    fetch_gain.wait()
    gains = gbuf[...]

    def settle(i, _):
        src = await_row(i)
        outv[src] = scaled(recv[src], gains, wsm[0, 0, src], wsm[0, 1, src])
        return 0
    lax.fori_loop(0, LATE, settle, 0)

    pltpu.make_async_copy(part_in, part_in, part_recv).wait()

    def gather_part(t, _):
        extra_in[:, pl.ds(pl.multiple_of(t * 128, 128), 128)] = part_in[lax.rem(bounded(ttab[1, 0], N) + 4 * t, N)]
        return 0
    lax.fori_loop(0, PIECES, gather_part, 0)
    outv[N] = scaled(extra_in[...], gains, wsm[1, 0, 0], wsm[1, 1, 0])
    lax.fori_loop(LATE, N, settle, 0)
    put = pltpu.make_async_copy(outv, rows_out, out_sem)
    put.start()

    drained(meta, meta_send)
    tiles = piece_in.at[pl.ds(0, PIECES - 1)]
    pltpu.make_async_copy(tiles, tiles, piece_send).wait()
    drained(part, part_send)
    drained(send, send_sem)
    put.wait()


def second(hidden, gain, prompt_of, weights, rows_out, hbuf, gbuf, tab, itab, stab, send, recv, wsm, outv,
           in_sem, tab_sem, send_sem, recv_sem, out_sem):
    me = my_place()
    barrier = greet_all(me)
    copies = [pltpu.make_async_copy(a, b, in_sem.at[k]) for k, (a, b) in enumerate(
        ((hidden, hbuf), (gain, gbuf), (prompt_of, tab.at[pl.ds(0, 1)]), (weights, wsm)))]
    for copy in copies:
        copy.start()
    for copy in copies:
        copy.wait()
    rows = lax.broadcasted_iota(jnp.int32, (N, N), 0)
    lanes = lax.broadcasted_iota(jnp.int32, (N, N), 1)
    lanef = lax.broadcasted_iota(jnp.int32, (8, N), 1).astype(jnp.float32)
    slot1 = slots_of(tab[0:1] // OWN, rows, jnp.where(rows < lanes, 1.0, 0.0))[1]
    itab[...] = dot(lanef, slot1, NT).astype(jnp.int32)
    to_scalar = pltpu.make_async_copy(itab, stab, tab_sem)
    to_scalar.start()
    to_scalar.wait()
    pl.semaphore_wait(barrier, N - 1)
    pack, ship, await_row, own = row_traffic(me, hbuf, stab, send, recv, send_sem, recv_sem)

    def pack_all(i, _):
        pack(i)
        return 0
    lax.fori_loop(0, N, pack_all, 0)
    own.start()

    def ship_all(i, _):
        ship(i)
        return 0
    lax.fori_loop(1, N, ship_all, 0)
    gains = gbuf[...]

    def settle(i, _):
        src = await_row(i)
        outv[src] = scaled(recv[src], gains, wsm[0, src], wsm[1, src])
        return 0
    lax.fori_loop(0, N, settle, 0)
    put = pltpu.make_async_copy(outv, rows_out, out_sem)
    put.start()
    drained(send, send_sem)
    put.wait()


def arrange(table, adv_in, rows_in, out, adv_out, buf, in_sem, out_sem):
    CH = 16

    def load(q, _):
        pltpu.make_async_copy(rows_in.at[bounded(table[0, q], rows_in.shape[0])], buf.at[q], in_sem.at[q // CH]).start()
        return 0
    lax.fori_loop(0, N, load, 0)
    adv_out[...] = adv_in[...]
    for c in range(N // CH):
        part = pl.ds(c * CH, CH)
        pltpu.make_async_copy(buf.at[part], buf.at[part], in_sem.at[c]).wait()
        pltpu.make_async_copy(buf.at[part], out.at[part], out_sem).start()
    pltpu.make_async_copy(buf, buf, out_sem).wait()


def on_device(hidden, norm_gain, prompt_of, lengths, reward_level):
    count, window, features = hidden.shape
    bf16, f32, i32 = jnp.bfloat16, jnp.float32, jnp.int32
    shape = jax.ShapeDtypeStruct
    any_space = pl.BlockSpec(memory_space=pl.ANY)
    vmem = pl.BlockSpec(memory_space=pltpu.VMEM)
    dma = pltpu.SemaphoreType.DMA
    block = pltpu.VMEM((N, window, features), bf16)
    square, strip = pltpu.VMEM((N, N), i32), pltpu.VMEM((8, N), i32)
    gains = pltpu.VMEM((1, features), f32)
    gain, prompt, length, level = (a.reshape(1, a.shape[0]) for a in (norm_gain, prompt_of, lengths, reward_level))
    rows, table, adv, weights = pl.pallas_call(
        exchange,
        out_shape=(shape((N + 1, window, features), bf16), shape((8, N), i32), shape((1, N), f32), shape((8, N), f32)),
        in_specs=[any_space] * 5,
        out_specs=(any_space, vmem, vmem, vmem),
        scratch_shapes=[
            block, gains, strip, strip, pltpu.SMEM((8, N), i32), strip, pltpu.SMEM((8, N), i32), square, square,
            pltpu.VMEM((window, features), bf16), pltpu.VMEM((PIECES, window, 128), bf16),
            pltpu.VMEM((N, window, 128), bf16), pltpu.VMEM((N, window, 128), bf16), pltpu.VMEM((window, features), bf16),
            block, block, pltpu.VMEM((2, 8, N), f32), pltpu.SMEM((2, 8, N), f32),
            pltpu.VMEM((N + 1, window, features), bf16),
            dma((5,)), dma((2,)), dma, dma, dma, dma, dma, dma, dma, dma((N,)), dma],
        compiler_params=pltpu.CompilerParams(collective_id=0, has_side_effects=True),
        name="exchange",
    )(hidden, gain, prompt, length, level)

    def place(table, adv, rows):
        return pl.pallas_call(
            arrange,
            out_shape=(shape((N, window, features), bf16), shape((1, N), f32)),
            in_specs=[pl.BlockSpec(memory_space=pltpu.SMEM), vmem, any_space],
            out_specs=(any_space, vmem),
            scratch_shapes=[block, dma((8,)), dma],
            name="arrange",
        )(table, adv, rows)

    def few(args):
        return place(table, adv, rows)

    def many(args):
        more = pl.pallas_call(
            second,
            out_shape=shape((N, window, features), bf16),
            in_specs=[any_space] * 4,
            out_specs=any_space,
            scratch_shapes=[
                block, gains, strip, strip, pltpu.SMEM((8, N), i32), block, block, pltpu.SMEM((8, N), f32), block,
                dma((4,)), dma, dma, dma((N,)), dma],
            compiler_params=pltpu.CompilerParams(collective_id=1, has_side_effects=True),
            name="second",
        )(hidden, gain, prompt, weights)
        return place(table[1:2], adv, jnp.concatenate([rows[:N], more]))

    out, adv = lax.cond(table[2, 0] > 1, many, few, 0)
    return out, adv.reshape(N)


def solution(mesh):
    spec = P(AXES)
    return jax.shard_map(
        on_device, mesh=mesh, in_specs=(P(AXES, None, None), P(), spec, spec, spec),
        out_specs=(P(AXES, None, None), spec), check_vma=False)
```

time: 76.6 us -> 64.8 us (0.85); the launches traced: 75.1 us -> 64.7 us
  Pallas kernels: 74.5 us -> 62.8 us
    pallas_call x2, Pallas kernels: 74.5 us -> 62.8 us  [the longest x1 56.2 us: on_device(): pl.pallas_call(exchange, out_shape=(shape((N + 1, window, features), bf16...]
where the time goes in v2:
time: 64.8 us; the launch traced here: 64.7 us
  Pallas kernels  62.8 us (97%)
  between operations  1.32 us (2%)
    pallas_call x1, Pallas kernels, on_device(): pl.pallas_call(exchange, out_shape=(shape((N + 1, window, features), bf16...  56.2 us
    pallas_call x1, Pallas kernels, place(): pl.pallas_call(arrange, out_shape=(shape((N, window, features), bf16), sh...  6.67 us

profile of v2, /device:TPU:1, one launch (start us, length us, event | category | flops | bytes accessed | tf_op | source)
XLA Modules:
  0.0 64.7 jit_solution(929799438446156129)
XLA Ops:
  0.6 0.0 copy-start
  0.6 0.0 copy-start.1
  0.7 56.2 %exchange.1 = (bf16[129,2,4096]{2,1,0:T(2,128)(2,1)S(1)}, s32[8,128]{1,0:T(8,128)S(1)}, f32[1,128]{1,0:T(1,128)S(1)}, f32[8,128]{1,0:T(8,128)S(1)}) custom-call(bf16[128,2,4096]{2,1,0:T(2,128)(2,1)} %hidden.1, f32[1,4096]{1,0:T(1,128)} %bitcast.7, s32[1,128]{1,0:T(1,128)} %bitcast.9, s32[1,128]{1,0:T(1,128)} %bitcast.11, s32[1,128]{1,0:T(1,128)} %bitcast.12), custom_call_target="tpu_custom_call" | custom-call | tf_op jit(solution)/shard_map/exchange/pallas_call | solution.py:356
  56.8 0.5 slice.9
  58.0 0.0 copy-done
  58.0 0.0 copy-done.1
  58.0 6.7 %conditional.1 = (bf16[128,2,4096]{2,1,0:T(2,128)(2,1)}, f32[128]{0:T(128)}) conditional(s32[]{:T(128)} %bitcast.6, (s32[8,128]{1,0:T(8,128)S(1)}, f32[1,128]{1,0:T(1,128)S(1)}, bf16[129,2,4096]{2,1,0:T(2,128)(2,1)S(1)}) %tuple.17, (s32[8,128]{1,0:T(8,128)S(1)}, bf16[129,2,4096]{2,1,0:T(2,128)(2,1)S(1)}, bf16[128,2,4096]{2,1,0:T(2,128)(2,1)}, ...), branch_computations={%region_0.0_spmd, %region_1.0_spmd} | conditional | flops 2097152 | bytes 12583952 | solution.py:399
  58.0 6.7 %arrange.2 = (bf16[128,2,4096]{2,1,0:T(2,128)(2,1)}, f32[1,128]{1,0:T(1,128)}) custom-call(s32[8,128]{1,0:T(8,128)S(1)} %get-tuple-element.25.table, f32[1,128]{1,0:T(1,128)S(1)} %get-tuple-element.26.adv_in, bf16[129,2,4096]{2,1,0:T(2,128)(2,1)S(1)} %get-tuple-element.27.rows_in), custom_call_target="tpu_custom_call" | custom-call | tf_op jit(solution)/shard_map/cond/branch_0_fun/arrange/pallas_call | solution.py:373
Async XLA Ops:
  0.6 57.4 %copy-start = (f32[4096]{0:T(1024)S(1)}, f32[4096]{0:T(1024)}, u32[]{:S(2)}) copy-start(f32[4096]{0:T(1024)} %param.8) | copy-start | bytes 49156
  0.6 57.4 %copy-start.1 = (s32[128]{0:T(128)S(1)}, s32[128]{0:T(128)}, u32[]{:S(2)}) copy-start(s32[128]{0:T(128)} %param.9) | copy-start | bytes 1540

commit v3 on v2

v3 whole, which is shorter than its diff:
```python
import functools

import jax
import jax.numpy as jnp
from jax import lax
from jax.experimental import pallas as pl
from jax.experimental.pallas import tpu as pltpu
from jax.sharding import PartitionSpec as P

LOGICAL = pl.DeviceIdType.LOGICAL
AXES = ("gx", "gy", "gz")
N = 128
G = 16
OWN = 8
PIECES = 32
EARLY = 48
LEAD = 4
BATCH = 8
LATE = 15
STRIDE = 37
norm_eps = 1e-05

NT = (((1,), (1,)), ((), ()))
NN = (((1,), (0,)), ((), ()))


def dot(a, b, dims, exact=False):
    if exact:
        return lax.dot_general(a, b, dims, precision=lax.Precision.HIGHEST,
                               preferred_element_type=jnp.float32)
    return lax.dot_general(a.astype(jnp.bfloat16), b.astype(jnp.bfloat16), dims,
                           preferred_element_type=jnp.float32)


class Place:
    def __init__(self):
        self.x, self.y, gz = lax.axis_index("gx"), lax.axis_index("gy"), lax.axis_index("gz")
        self.z, self.core = gz // 2, lax.rem(gz, 2)
        self.me = self.x * 32 + self.y * 8 + gz
        self.xs = [lax.rem(self.x + k, 4) * 32 for k in range(4)]
        self.ys = [lax.rem(self.y + k, 4) * 8 for k in range(4)]
        self.zs = [lax.rem(self.z + k, 4) * 2 for k in range(4)]
        self.cores = [lax.rem(self.core + k, 2) for k in range(2)]
        self.zc = [[z + c for c in self.cores] for z in self.zs]
        self.xy = [[a + b for b in self.ys] for a in self.xs]

    def target(self, i):
        o = (i * STRIDE) % N
        return self.xy[o // 32][o // 8 % 4] + self.zc[o // 2 % 4][o % 2]

    def target_of(self, i):
        o = lax.rem(i * STRIDE, N)
        return (lax.rem(self.x + o // 32, 4) * 32 + lax.rem(self.y + lax.rem(o // 8, 4), 4) * 8
                + lax.rem(self.z + lax.rem(o // 2, 4), 4) * 2 + lax.rem(self.core + lax.rem(o, 2), 2))

    def all(self, i, sign):
        o = (i * STRIDE) & (N - 1)
        return ((((self.x + sign * (o >> 5)) & 3) << 5) + (((self.y + sign * ((o >> 3) & 3)) & 3) << 3)
                + (((self.z + sign * ((o >> 1) & 3)) & 3) << 1) + ((self.core + o) & 1))

    def greet(self):
        barrier = pltpu.get_barrier_semaphore()
        for i in range(1, N):
            pl.semaphore_signal(barrier, inc=1, device_id=self.target(i), device_id_type=LOGICAL)
        return barrier


def ints(shape, dim):
    return lax.broadcasted_iota(jnp.int32, shape, dim)


def split(owner, target, ahead):
    mine = owner == target
    earlier = dot(jnp.where(mine, 1.0, 0.0), ahead, NN)
    return jnp.where(mine & (earlier < 0.5), 1.0, 0.0), jnp.where(mine & (earlier == 1.0), 1.0, 0.0)


def bounded(i, n):
    return jnp.clip(i, 0, n - 1)


def scaled(x, gains, w0, w1):
    token = ints((2, 1), 0)
    x = x.astype(jnp.float32)
    meansq = jnp.mean(x * x, axis=-1, keepdims=True)
    y = (x * lax.rsqrt(meansq + norm_eps) * gains).astype(jnp.bfloat16)
    return (y.astype(jnp.float32) * jnp.where(token == 0, w0, w1)).astype(jnp.bfloat16)


def whole(ref, sem):
    return pltpu.make_async_copy(ref, ref, sem)


def remote(src, dst, send_sem, recv_sem, to):
    return pltpu.make_async_remote_copy(src_ref=src, dst_ref=dst, send_sem=send_sem, recv_sem=recv_sem,
                                        device_id=to, device_id_type=LOGICAL)


def exchange(hidden, gain, prompt_of, lengths, reward, rows_out, table_out, flag_out, adv_out, weights_out,
             hbuf, gbuf, tab, itab, stab, jtab, ttab, meta, meta_in, extra, piece_in, part, part_in, extra_in,
             send, recv, wtab, wsm,
             in_sem, tab_sem, meta_send, meta_recv, piece_send, piece_recv, part_send, part_recv,
             send_sem, recv_sem):
    fetch_tab = [pltpu.make_async_copy(ref, tab.at[pl.ds(k, 1)], in_sem.at[2 + k])
                 for k, ref in enumerate((prompt_of, lengths, reward))]
    fetch_rows = pltpu.make_async_copy(hidden, hbuf, in_sem.at[0])
    fetch_gain = pltpu.make_async_copy(gain, gbuf, in_sem.at[1])
    for copy in fetch_tab:
        copy.start()
    fetch_rows.start()
    fetch_gain.start()
    place = Place()
    me = place.me
    barrier = place.greet()
    for copy in fetch_tab:
        copy.wait()

    rows, lanes = ints((N, N), 0), ints((N, N), 1)
    row8, lane8 = ints((8, N), 0), ints((8, N), 1)
    lane1 = ints((1, N), 1)
    lanef = lane8.astype(jnp.float32)
    target = place.all(rows, 1)

    prompt, length, level = tab[0:1], tab[1:2], tab[2:3]
    owner, label = prompt // OWN, lax.rem(prompt, OWN) + 1
    slot0, slot1 = split(owner, target, jnp.where(rows < lanes, 1.0, 0.0))
    twice = jnp.sum(slot1, axis=0, keepdims=True)
    spare = jnp.sum(twice, axis=1, keepdims=True)
    spare_row = jnp.sum(twice * lane1.astype(jnp.float32), axis=1, keepdims=True)
    spare_to = jnp.where(spare > 0.5, jnp.sum(twice * owner.astype(jnp.float32), axis=1, keepdims=True), -1.0)
    itab[...] = jnp.where(row8 == 0, dot(lanef, slot0, NT), spare_row).astype(jnp.int32)
    to_scalar = pltpu.make_async_copy(itab, stab, tab_sem.at[0])
    to_scalar.start()
    zero = jnp.zeros((N, N), jnp.int32)
    told = jnp.where(rows == 0, label, jnp.where(rows == 1, level, jnp.where(rows == 2, length, zero)))
    told1 = jnp.where(rows == 3, label, jnp.where(rows == 4, level, jnp.where(rows == 5, length, zero)))
    meta[...] = (dot(slot0, told.astype(jnp.float32), NT) + dot(slot1, told1.astype(jnp.float32), NT)
                 + jnp.where(lanes == 6, spare_to, jnp.where(lanes == 7, spare, 0.0))).astype(jnp.int32)
    to_scalar.wait()
    fetch_rows.wait()
    extra[...] = hbuf[bounded(stab[1, 0], N)]

    def pack(i):
        send[i] = hbuf[bounded(stab[0, i], N)]

    def ship(i):
        remote(send.at[i], recv.at[i], send_sem, recv_sem.at[i // BATCH], place.target(i)).start()

    for i in range(LEAD + 1):
        pack(i)
    own = pltpu.make_async_copy(send.at[0], recv.at[0], recv_sem.at[0])
    own_meta = pltpu.make_async_copy(meta.at[pl.ds(0, 1)], meta_in.at[pl.ds(0, 1)], meta_recv)
    own_piece = pltpu.make_async_copy(extra.at[:, pl.ds(0, 128)], piece_in.at[me // 4], piece_recv)
    own.start()
    own_meta.start()
    own_piece.start()

    pl.semaphore_wait(barrier, N - 1)

    for i in range(1, N):
        remote(meta.at[pl.ds(i, 1)], meta_in.at[pl.ds(i, 1)], meta_send, meta_recv, place.target(i)).start()
    for t in range(1, PIECES):
        remote(extra.at[:, pl.ds(t * 128, 128)], piece_in.at[me // 4], piece_send, piece_recv,
               lax.rem(me + 4 * t, N)).start()
    for i in range(1, EARLY):
        pack(i + LEAD)
        ship(i)

    whole(meta_in, meta_recv).wait()
    told_in = meta_in[...].astype(jnp.float32)
    by_step = dot(jnp.where(row8 == lane8, 1.0, 0.0), told_in, NT)
    label0, label1, to1, spares = by_step[0:1], by_step[3:4], by_step[6:7], by_step[7:8]
    source = place.all(lane1, -1)

    goes = to1 == target.astype(jnp.float32)
    passing = jnp.where(goes & (lax.rem(source, 4) == lax.rem(me, 4)), 1.0, 0.0)
    piece_of = dot((place.all(lane8, -1) // 4).astype(jnp.float32), passing, NT)
    here = jnp.where(to1 == me.astype(jnp.float32), 1.0, 0.0)
    giver = jnp.sum(here * source.astype(jnp.float32), axis=1, keepdims=True)
    jtab[...] = jnp.where(row8 == 0, piece_of, giver).astype(jnp.int32)
    to_scalar = pltpu.make_async_copy(jtab, ttab, tab_sem.at[0])
    to_scalar.start()

    ahead = jnp.where(place.all(rows, -1) < source, 1.0, 0.0)
    group = (rows // G + 1).astype(jnp.float32)
    rank = lax.rem(rows, G).astype(jnp.float32)
    in0, in1 = jnp.where(label0 == group, 1.0, 0.0), jnp.where(label1 == group, 1.0, 0.0)
    passed = dot(in0 + in1, ahead, NN)
    take0 = jnp.where((in0 > 0.5) & (passed == rank), 1.0, 0.0)
    take1 = jnp.where((in1 > 0.5) & (passed + in0 == rank), 1.0, 0.0)

    to_scalar.wait()
    whole(piece_in, piece_recv).wait()
    for i in range(N):
        part[i] = piece_in[bounded(ttab[0, i], PIECES)]

    crowd = jnp.sum(jnp.where(goes, 1.0, 0.0), axis=1, keepdims=True)
    worst = jnp.maximum(jnp.max(crowd, axis=0, keepdims=True), jnp.max(spares, axis=1, keepdims=True))
    facts0 = jnp.where(row8 == 0, by_step[1:2], jnp.where(row8 == 1, by_step[2:3], lanef))
    facts1 = jnp.where(row8 == 0, by_step[4:5], jnp.where(row8 == 1, by_step[5:6], jnp.where(row8 == 2, 1.0 * N, lanef + N)))
    facts = dot(facts0, take0, NT) + dot(facts1, take1, NT)

    own_part = pltpu.make_async_copy(part.at[0], part_in.at[me], part_recv)
    own_part.start()
    for i in range(1, N):
        remote(part.at[i], part_in.at[me], part_send, part_recv, place.target(i)).start()
    for i in range(EARLY, N):
        if i + LEAD < N:
            pack(i + LEAD)
        ship(i)

    same = jnp.where(rows // G == lanes // G, 1.0, 0.0)
    mean = dot(facts, same, NN) * (1.0 / G)
    centred = facts - mean
    spread = jnp.sqrt(dot(centred * centred, same, NN, exact=True) * (1.0 / G))
    adv = centred[0:1] / jnp.maximum(spread[0:1], 1.0)
    count = facts[1:2]
    weight = adv / count
    wrows = jnp.where(row8 == 0, weight, jnp.where((row8 == 1) & (count > 1.5), weight, 0.0))
    by0, by1 = dot(wrows, take0, NN, exact=True), dot(wrows, take1, NN, exact=True)
    wtab[0] = by0
    wtab[1] = jnp.sum(by1 * here, axis=1, keepdims=True) + jnp.zeros((8, N), jnp.float32)
    to_scalar = pltpu.make_async_copy(wtab, wsm, tab_sem.at[1])
    to_scalar.start()
    weights_out[...] = by1
    table_out[...] = jnp.where(row8 == 0, facts[2:3], facts[3:4]).astype(jnp.int32)
    flag_out[...] = worst.astype(jnp.int32)
    adv_out[...] = adv
    to_scalar.wait()
    fetch_gain.wait()
    gains = gbuf[...]

    def settle(g, _):
        whole(recv.at[pl.ds(0, BATCH)], recv_sem.at[g]).wait()
        for k in range(BATCH):
            i = g * BATCH + k
            rows_out[i] = scaled(recv[i], gains, wsm[0, 0, i], wsm[0, 1, i])
        return 0
    lax.fori_loop(0, LATE, settle, 0)

    whole(part_in, part_recv).wait()
    giver = bounded(ttab[1, 0], N)
    for t in range(PIECES):
        extra_in[:, pl.ds(t * 128, 128)] = part_in[lax.rem(giver + 4 * t, N)]
    rows_out[N] = scaled(extra_in[...], gains, wsm[1, 0, 0], wsm[1, 1, 0])
    lax.fori_loop(LATE, N // BATCH, settle, 0)

    whole(meta.at[pl.ds(0, N - 1)], meta_send).wait()
    whole(piece_in.at[pl.ds(0, PIECES - 1)], piece_send).wait()
    whole(part.at[pl.ds(0, N - 1)], part_send).wait()
    whole(send.at[pl.ds(0, N - 1)], send_sem).wait()


def second(hidden, gain, prompt_of, weights, rows_out, hbuf, gbuf, tab, itab, stab, send, recv, wsm, outv,
           in_sem, tab_sem, send_sem, recv_sem, out_sem):
    copies = [pltpu.make_async_copy(a, b, in_sem.at[k]) for k, (a, b) in enumerate(
        ((hidden, hbuf), (gain, gbuf), (prompt_of, tab.at[pl.ds(0, 1)]), (weights, wsm)))]
    for copy in copies:
        copy.start()
    place = Place()
    barrier = place.greet()
    for copy in copies:
        copy.wait()
    rows, lanes = ints((N, N), 0), ints((N, N), 1)
    slot1 = split(tab[0:1] // OWN, place.all(rows, 1), jnp.where(rows < lanes, 1.0, 0.0))[1]
    itab[...] = dot(ints((8, N), 1).astype(jnp.float32), slot1, NT).astype(jnp.int32)
    to_scalar = pltpu.make_async_copy(itab, stab, tab_sem)
    to_scalar.start()
    to_scalar.wait()
    pl.semaphore_wait(barrier, N - 1)

    def pack(i, _):
        send[i] = hbuf[bounded(stab[0, i], N)]
        return 0
    lax.fori_loop(0, N, pack, 0)
    pltpu.make_async_copy(send.at[0], recv.at[0], recv_sem).start()

    def ship(i, _):
        remote(send.at[i], recv.at[i], send_sem, recv_sem, place.target_of(i)).start()
        return 0
    lax.fori_loop(1, N, ship, 0)
    whole(recv, recv_sem).wait()
    gains = gbuf[...]

    def settle(i, _):
        outv[i] = scaled(recv[i], gains, wsm[0, i], wsm[1, i])
        return 0
    lax.fori_loop(0, N, settle, 0)
    whole(send.at[pl.ds(0, N - 1)], send_sem).wait()
    put = pltpu.make_async_copy(outv, rows_out, out_sem)
    put.start()
    put.wait()


def arrange(table, adv_in, rows_in, out, adv_out, sem):
    for q in range(N):
        pltpu.make_async_copy(rows_in.at[bounded(table[0, q], rows_in.shape[0])], out.at[q], sem).start()
    adv_out[...] = adv_in[...]
    whole(out, sem).wait()


def on_device(hidden, norm_gain, prompt_of, lengths, reward_level):
    count, window, features = hidden.shape
    bf16, f32, i32 = jnp.bfloat16, jnp.float32, jnp.int32
    shape = jax.ShapeDtypeStruct
    any_space = pl.BlockSpec(memory_space=pl.ANY)
    vmem = pl.BlockSpec(memory_space=pltpu.VMEM)
    dma = pltpu.SemaphoreType.DMA
    block = pltpu.VMEM((N, window, features), bf16)
    square, strip = pltpu.VMEM((N, N), i32), pltpu.VMEM((8, N), i32)
    gains = pltpu.VMEM((1, features), f32)
    gain, prompt, length, level = (a.reshape(1, a.shape[0]) for a in (norm_gain, prompt_of, lengths, reward_level))
    rows, table, flag, adv, weights = pl.pallas_call(
        exchange,
        out_shape=(shape((N + 1, window, features), bf16), shape((8, N), i32), shape((1, 1), i32),
                   shape((1, N), f32), shape((8, N), f32)),
        in_specs=[any_space] * 5,
        out_specs=(vmem,) * 5,
        scratch_shapes=[
            block, gains, strip, strip, pltpu.SMEM((8, N), i32), strip, pltpu.SMEM((8, N), i32), square, square,
            pltpu.VMEM((window, features), bf16), pltpu.VMEM((PIECES, window, 128), bf16),
            pltpu.VMEM((N, window, 128), bf16), pltpu.VMEM((N, window, 128), bf16), pltpu.VMEM((window, features), bf16),
            block, block, pltpu.VMEM((2, 8, N), f32), pltpu.SMEM((2, 8, N), f32),
            dma((5,)), dma((2,)), dma, dma, dma, dma, dma, dma, dma, dma((N // BATCH,))],
        compiler_params=pltpu.CompilerParams(collective_id=0, has_side_effects=True),
        name="exchange",
    )(hidden, gain, prompt, length, level)

    def put(table, adv, rows):
        return pl.pallas_call(
            arrange,
            out_shape=(shape((N, window, features), bf16), shape((1, N), f32)),
            in_specs=[pl.BlockSpec(memory_space=pltpu.SMEM), vmem, any_space],
            out_specs=(any_space, vmem),
            scratch_shapes=[dma],
            name="arrange",
        )(table, adv, rows)

    def few(_):
        return put(table, adv, rows)

    def many(_):
        more = pl.pallas_call(
            second,
            out_shape=shape((N, window, features), bf16),
            in_specs=[any_space] * 4,
            out_specs=any_space,
            scratch_shapes=[
                block, gains, strip, strip, pltpu.SMEM((8, N), i32), block, block, pltpu.SMEM((8, N), f32), block,
                dma((4,)), dma, dma, dma, dma],
            compiler_params=pltpu.CompilerParams(collective_id=1, has_side_effects=True),
            name="second",
        )(hidden, gain, prompt, weights)
        return put(table[1:2], adv, jnp.concatenate([rows[:N], more]))

    out, adv = lax.cond(flag[0, 0] > 1, many, few, 0)
    return out, adv.reshape(N)


def solution(mesh):
    spec = P(AXES)
    return jax.shard_map(
        on_device, mesh=mesh, in_specs=(P(AXES, None, None), P(), spec, spec, spec),
        out_specs=(P(AXES, None, None), spec), check_vma=False)
```

time: 64.8 us -> 44.1 us (0.68)
  Pallas kernels: 62.8 us -> 42.2 us
    pallas_call x1, Pallas kernels: 56.2 us -> 39.8 us  [on_device(): pl.pallas_call(exchange, out_shape=(shape((N + 1, window, features), bf16...]
    pallas_call x1, Pallas kernels: 6.67 us -> 2.4 us  [put(): pl.pallas_call(arrange, out_shape=(shape((N, window, features), bf16), sh...]
where the time goes in v3:
time: 44.1 us; the launch traced here: 44 us
  Pallas kernels  42.2 us (96%)
  between operations  1.52 us (3%)
    pallas_call x1, Pallas kernels, on_device(): pl.pallas_call(exchange, out_shape=(shape((N + 1, window, features), bf16...  39.8 us
    pallas_call x1, Pallas kernels, put(): pl.pallas_call(arrange, out_shape=(shape((N, window, features), bf16), sh...  2.4 us

profile of v3, /device:TPU:1, one launch (start us, length us, event | category | flops | bytes accessed | tf_op | source)
XLA Modules:
  0.0 44.0 jit_solution(2724210402280743230)
XLA Ops:
  0.6 0.0 copy-start
  0.6 0.0 copy-start.1
  0.7 39.8 %exchange.1 = (bf16[129,2,4096]{2,1,0:T(2,128)(2,1)S(1)}, s32[8,128]{1,0:T(8,128)S(1)}, s32[1,1]{1,0:T(1,128)}, f32[1,128]{1,0:T(1,128)S(1)}, f32[8,128]{1,0:T(8,128)S(1)}) custom-call(bf16[128,2,4096]{2,1,0:T(2,128)(2,1)} %hidden.1, f32[1,4096]{1,0:T(1,128)} %bitcast.7, s32[1,128]{1,0:T(1,128)} %bitcast.9, s32[1,128]{1,0:T(1,128)} %bitcast.11, ...), custom_call_target="tpu_custom_call" | custom-call | tf_op jit(solution)/shard_map/exchange/pallas_call | solution.py:313
  41.2 0.0 copy-done
  41.2 0.0 copy-done.1
  41.2 2.6 %conditional.1 = (bf16[128,2,4096]{2,1,0:T(2,128)(2,1)}, f32[128]{0:T(128)}) conditional(s32[]{:T(128)} %bitcast.6, (s32[8,128]{1,0:T(8,128)S(1)}, f32[1,128]{1,0:T(1,128)S(1)}, bf16[129,2,4096]{2,1,0:T(2,128)(2,1)S(1)}) %tuple.17, (s32[8,128]{1,0:T(8,128)S(1)}, bf16[129,2,4096]{2,1,0:T(2,128)(2,1)S(1)}, bf16[128,2,4096]{2,1,0:T(2,128)(2,1)}, ...), branch_computations={%region_0.0_spmd, %region_1.0_spmd} | conditional | flops 2097152 | bytes 12583952 | solution.py:356
  41.2 2.4 %arrange.2 = (bf16[128,2,4096]{2,1,0:T(2,128)(2,1)}, f32[1,128]{1,0:T(1,128)}) custom-call(s32[8,128]{1,0:T(8,128)S(1)} %get-tuple-element.25.table, f32[1,128]{1,0:T(1,128)S(1)} %get-tuple-element.26.adv_in, bf16[129,2,4096]{2,1,0:T(2,128)(2,1)S(1)} %get-tuple-element.27.rows_in), custom_call_target="tpu_custom_call" | custom-call | tf_op jit(solution)/shard_map/cond/branch_0_fun/arrange/pallas_call | solution.py:330
Async XLA Ops:
  0.6 40.6 %copy-start = (f32[4096]{0:T(1024)S(1)}, f32[4096]{0:T(1024)}, u32[]{:S(2)}) copy-start(f32[4096]{0:T(1024)} %param.8) | copy-start | bytes 49156
  0.6 40.6 %copy-start.1 = (s32[128]{0:T(128)S(1)}, s32[128]{0:T(128)}, u32[]{:S(2)}) copy-start(s32[128]{0:T(128)} %param.9) | copy-start | bytes 1540

commit v4 on v3

--- a/solution.py
+++ b/solution.py
@@ -15,6 +15,8 @@
 PIECES = 32
 EARLY = 48
 LEAD = 4
+FIRST = 8
+READY = 16
 BATCH = 8
 LATE = 15
 STRIDE = 37
@@ -30,6 +32,11 @@
                                preferred_element_type=jnp.float32)
     return lax.dot_general(a.astype(jnp.bfloat16), b.astype(jnp.bfloat16), dims,
                            preferred_element_type=jnp.float32)
+
+
+def hops(i):
+    o = (i * STRIDE) % N
+    return sum(min(k, 4 - k) for k in (o // 32, o // 8 % 4, o // 2 % 4))
 
 
 class Place:
@@ -60,7 +67,7 @@
 
     def greet(self):
         barrier = pltpu.get_barrier_semaphore()
-        for i in range(1, N):
+        for i in sorted(range(1, N), key=hops, reverse=True):
             pl.semaphore_signal(barrier, inc=1, device_id=self.target(i), device_id_type=LOGICAL)
         return barrier
 
@@ -79,12 +86,14 @@
     return jnp.clip(i, 0, n - 1)
 
 
-def scaled(x, gains, w0, w1):
-    token = ints((2, 1), 0)
+def normed(x, gains):
     x = x.astype(jnp.float32)
     meansq = jnp.mean(x * x, axis=-1, keepdims=True)
-    y = (x * lax.rsqrt(meansq + norm_eps) * gains).astype(jnp.bfloat16)
-    return (y.astype(jnp.float32) * jnp.where(token == 0, w0, w1)).astype(jnp.bfloat16)
+    return (x * lax.rsqrt(meansq + norm_eps) * gains).astype(jnp.bfloat16)
+
+
+def weighed(y, w0, w1):
+    return (y.astype(jnp.float32) * jnp.where(ints((2, 1), 0) == 0, w0, w1)).astype(jnp.bfloat16)
 
 
 def whole(ref, sem):
@@ -98,7 +107,7 @@
 
 def exchange(hidden, gain, prompt_of, lengths, reward, rows_out, table_out, flag_out, adv_out, weights_out,
              hbuf, gbuf, tab, itab, stab, jtab, ttab, meta, meta_in, extra, piece_in, part, part_in, extra_in,
-             send, recv, wtab, wsm,
+             send, recv, wtab, wsm, flag,
              in_sem, tab_sem, meta_send, meta_recv, piece_send, piece_recv, part_send, part_recv,
              send_sem, recv_sem):
     fetch_tab = [pltpu.make_async_copy(ref, tab.at[pl.ds(k, 1)], in_sem.at[2 + k])
@@ -137,33 +146,48 @@
     meta[...] = (dot(slot0, told.astype(jnp.float32), NT) + dot(slot1, told1.astype(jnp.float32), NT)
                  + jnp.where(lanes == 6, spare_to, jnp.where(lanes == 7, spare, 0.0))).astype(jnp.int32)
     to_scalar.wait()
+    fetch_gain.wait()
+    gains = gbuf[...]
     fetch_rows.wait()
-    extra[...] = hbuf[bounded(stab[1, 0], N)]
+    extra[...] = normed(hbuf[bounded(stab[1, 0], N)], gains)
 
     def pack(i):
-        send[i] = hbuf[bounded(stab[0, i], N)]
+        if i < N:
+            send[i] = normed(hbuf[bounded(stab[0, i], N)], gains)
 
     def ship(i):
         remote(send.at[i], recv.at[i], send_sem, recv_sem.at[i // BATCH], place.target(i)).start()
 
-    for i in range(LEAD + 1):
+    def hand(r):
+        t = lax.rem(me // 4 + r, PIECES)
+        return extra.at[:, pl.ds(pl.multiple_of(t * 128, 128), 128)], 4 * t
+
+    relay = lax.rem(me, 4) == 0
+    for i in range(READY):
         pack(i)
-    own = pltpu.make_async_copy(send.at[0], recv.at[0], recv_sem.at[0])
-    own_meta = pltpu.make_async_copy(meta.at[pl.ds(0, 1)], meta_in.at[pl.ds(0, 1)], meta_recv)
-    own_piece = pltpu.make_async_copy(extra.at[:, pl.ds(0, 128)], piece_in.at[me // 4], piece_recv)
-    own.start()
-    own_meta.start()
-    own_piece.start()
+    pltpu.make_async_copy(send.at[0], recv.at[0], recv_sem.at[0]).start()
+    pltpu.make_async_copy(meta.at[pl.ds(0, 1)], meta_in.at[pl.ds(0, 1)], meta_recv).start()
+
+    @pl.when(relay)
+    def _():
+        pltpu.make_async_copy(hand(0)[0], piece_in.at[me], piece_recv).start()
 
     pl.semaphore_wait(barrier, N - 1)
 
+    for i in range(1, FIRST):
+        ship(i)
     for i in range(1, N):
         remote(meta.at[pl.ds(i, 1)], meta_in.at[pl.ds(i, 1)], meta_send, meta_recv, place.target(i)).start()
-    for t in range(1, PIECES):
-        remote(extra.at[:, pl.ds(t * 128, 128)], piece_in.at[me // 4], piece_send, piece_recv,
-               lax.rem(me + 4 * t, N)).start()
-    for i in range(1, EARLY):
-        pack(i + LEAD)
+
+    @pl.when(jnp.logical_not(relay))
+    def _():
+        tile, to = hand(0)
+        remote(tile, piece_in.at[me], piece_send, piece_recv, to).start()
+    for r in range(1, PIECES):
+        tile, to = hand(r)
+        remote(tile, piece_in.at[me], piece_send, piece_recv, to).start()
+    for i in range(FIRST, EARLY):
+        pack(i - FIRST + READY)
         ship(i)
 
     whole(meta_in, meta_recv).wait()
@@ -173,13 +197,10 @@
     source = place.all(lane1, -1)
 
     goes = to1 == target.astype(jnp.float32)
-    passing = jnp.where(goes & (lax.rem(source, 4) == lax.rem(me, 4)), 1.0, 0.0)
-    piece_of = dot((place.all(lane8, -1) // 4).astype(jnp.float32), passing, NT)
-    here = jnp.where(to1 == me.astype(jnp.float32), 1.0, 0.0)
-    giver = jnp.sum(here * source.astype(jnp.float32), axis=1, keepdims=True)
-    jtab[...] = jnp.where(row8 == 0, piece_of, giver).astype(jnp.int32)
+    jtab[...] = dot(place.all(lane8, -1).astype(jnp.float32), jnp.where(goes, 1.0, 0.0), NT).astype(jnp.int32)
     to_scalar = pltpu.make_async_copy(jtab, ttab, tab_sem.at[0])
     to_scalar.start()
+    here = jnp.where(to1 == me.astype(jnp.float32), 1.0, 0.0)
 
     ahead = jnp.where(place.all(rows, -1) < source, 1.0, 0.0)
     group = (rows // G + 1).astype(jnp.float32)
@@ -189,24 +210,34 @@
     take0 = jnp.where((in0 > 0.5) & (passed == rank), 1.0, 0.0)
     take1 = jnp.where((in1 > 0.5) & (passed + in0 == rank), 1.0, 0.0)
 
-    to_scalar.wait()
-    whole(piece_in, piece_recv).wait()
-    for i in range(N):
-        part[i] = piece_in[bounded(ttab[0, i], PIECES)]
-
     crowd = jnp.sum(jnp.where(goes, 1.0, 0.0), axis=1, keepdims=True)
     worst = jnp.maximum(jnp.max(crowd, axis=0, keepdims=True), jnp.max(spares, axis=1, keepdims=True))
     facts0 = jnp.where(row8 == 0, by_step[1:2], jnp.where(row8 == 1, by_step[2:3], lanef))
     facts1 = jnp.where(row8 == 0, by_step[4:5], jnp.where(row8 == 1, by_step[5:6], jnp.where(row8 == 2, 1.0 * N, lanef + N)))
     facts = dot(facts0, take0, NT) + dot(facts1, take1, NT)
 
-    own_part = pltpu.make_async_copy(part.at[0], part_in.at[me], part_recv)
-    own_part.start()
-    for i in range(1, N):
-        remote(part.at[i], part_in.at[me], part_send, part_recv, place.target(i)).start()
-    for i in range(EARLY, N):
-        if i + LEAD < N:
-            pack(i + LEAD)
+    flag[...] = worst.astype(jnp.int32)
+    flag_copy = pltpu.make_async_copy(flag, flag_out, in_sem.at[0])
+    flag_copy.start()
+    to_scalar.wait()
+
+    @pl.when(relay)
+    def _():
+        whole(piece_in, piece_recv).wait()
+        for i in range(N):
+            part[i] = piece_in[bounded(ttab[0, i], N)]
+        for i in range(EARLY, EARLY + LEAD):
+            ship(i)
+        pltpu.make_async_copy(part.at[0], part_in.at[me // 4], part_recv).start()
+        for i in range(1, N):
+            remote(part.at[i], part_in.at[me // 4], part_send, part_recv, place.target(i)).start()
+
+    @pl.when(jnp.logical_not(relay))
+    def _():
+        for i in range(EARLY, EARLY + LEAD):
+            ship(i)
+    for i in range(EARLY + LEAD, N):
+        pack(i - FIRST - LEAD + READY)
         ship(i)
 
     same = jnp.where(rows // G == lanes // G, 1.0, 0.0)
@@ -224,31 +255,35 @@
     to_scalar.start()
     weights_out[...] = by1
     table_out[...] = jnp.where(row8 == 0, facts[2:3], facts[3:4]).astype(jnp.int32)
-    flag_out[...] = worst.astype(jnp.int32)
     adv_out[...] = adv
     to_scalar.wait()
-    fetch_gain.wait()
-    gains = gbuf[...]
 
     def settle(g, _):
         whole(recv.at[pl.ds(0, BATCH)], recv_sem.at[g]).wait()
         for k in range(BATCH):
             i = g * BATCH + k
-            rows_out[i] = scaled(recv[i], gains, wsm[0, 0, i], wsm[0, 1, i])
+            rows_out[i] = weighed(recv[i], wsm[0, 0, i], wsm[0, 1, i])
         return 0
     lax.fori_loop(0, LATE, settle, 0)
 
     whole(part_in, part_recv).wait()
-    giver = bounded(ttab[1, 0], N)
     for t in range(PIECES):
-        extra_in[:, pl.ds(t * 128, 128)] = part_in[lax.rem(giver + 4 * t, N)]
-    rows_out[N] = scaled(extra_in[...], gains, wsm[1, 0, 0], wsm[1, 1, 0])
+        extra_in[:, pl.ds(t * 128, 128)] = part_in[t]
+    rows_out[N] = weighed(extra_in[...], wsm[1, 0, 0], wsm[1, 1, 0])
     lax.fori_loop(LATE, N // BATCH, settle, 0)
 
     whole(meta.at[pl.ds(0, N - 1)], meta_send).wait()
-    whole(piece_in.at[pl.ds(0, PIECES - 1)], piece_send).wait()
-    whole(part.at[pl.ds(0, N - 1)], part_send).wait()
     whole(send.at[pl.ds(0, N - 1)], send_sem).wait()
+    flag_copy.wait()
+
+    @pl.when(relay)
+    def _():
+        whole(piece_in.at[pl.ds(0, PIECES - 1)], piece_send).wait()
+        whole(part.at[pl.ds(0, N - 1)], part_send).wait()
+
+    @pl.when(jnp.logical_not(relay))
+    def _():
+        whole(piece_in.at[pl.ds(0, PIECES)], piece_send).wait()
 
 
 def second(hidden, gain, prompt_of, weights, rows_out, hbuf, gbuf, tab, itab, stab, send, recv, wsm, outv,
@@ -283,7 +318,7 @@
     gains = gbuf[...]
 
     def settle(i, _):
-        outv[i] = scaled(recv[i], gains, wsm[0, i], wsm[1, i])
+        outv[i] = weighed(normed(recv[i], gains), wsm[0, i], wsm[1, i])
         return 0
     lax.fori_loop(0, N, settle, 0)
     whole(send.at[pl.ds(0, N - 1)], send_sem).wait()
@@ -315,12 +350,12 @@
         out_shape=(shape((N + 1, window, features), bf16), shape((8, N), i32), shape((1, 1), i32),
                    shape((1, N), f32), shape((8, N), f32)),
         in_specs=[any_space] * 5,
-        out_specs=(vmem,) * 5,
+        out_specs=(vmem, vmem, any_space, vmem, vmem),
         scratch_shapes=[
             block, gains, strip, strip, pltpu.SMEM((8, N), i32), strip, pltpu.SMEM((8, N), i32), square, square,
-            pltpu.VMEM((window, features), bf16), pltpu.VMEM((PIECES, window, 128), bf16),
-            pltpu.VMEM((N, window, 128), bf16), pltpu.VMEM((N, window, 128), bf16), pltpu.VMEM((window, features), bf16),
-            block, block, pltpu.VMEM((2, 8, N), f32), pltpu.SMEM((2, 8, N), f32),
+            pltpu.VMEM((window, features), bf16), pltpu.VMEM((N, window, 128), bf16),
+            pltpu.VMEM((N, window, 128), bf16), pltpu.VMEM((PIECES, window, 128), bf16), pltpu.VMEM((window, features), bf16),
+            block, block, pltpu.VMEM((2, 8, N), f32), pltpu.SMEM((2, 8, N), f32), pltpu.VMEM((1, 1), i32),
             dma((5,)), dma((2,)), dma, dma, dma, dma, dma, dma, dma, dma((N // BATCH,))],
         compiler_params=pltpu.CompilerParams(collective_id=0, has_side_effects=True),
         name="exchange",

time: 44.1 us -> 42.5 us (0.964)
  Pallas kernels: 42.2 us -> 40.7 us
    pallas_call x1, Pallas kernels: 39.8 us -> 38.3 us  [on_device(): pl.pallas_call(exchange, out_shape=(shape((N + 1, window, features), bf16...]
where the time goes in v4:
time: 42.5 us; the launch traced here: 42.4 us
  Pallas kernels  40.7 us (96%)
  between operations  1.52 us (4%)
    pallas_call x1, Pallas kernels, on_device(): pl.pallas_call(exchange, out_shape=(shape((N + 1, window, features), bf16...  38.3 us
    pallas_call x1, Pallas kernels, put(): pl.pallas_call(arrange, out_shape=(shape((N, window, features), bf16), sh...  2.4 us

profile of v4, /device:TPU:1, one launch (start us, length us, event | category | flops | bytes accessed | tf_op | source)
XLA Modules:
  0.0 42.4 jit_solution(4637041346139345983)
XLA Ops:
  0.6 0.0 copy-start
  0.6 0.0 copy-start.1
  0.7 38.3 %exchange.1 = (bf16[129,2,4096]{2,1,0:T(2,128)(2,1)S(1)}, s32[8,128]{1,0:T(8,128)S(1)}, s32[1,1]{1,0:T(1,128)}, f32[1,128]{1,0:T(1,128)S(1)}, f32[8,128]{1,0:T(8,128)S(1)}) custom-call(bf16[128,2,4096]{2,1,0:T(2,128)(2,1)} %hidden.1, f32[1,4096]{1,0:T(1,128)} %bitcast.7, s32[1,128]{1,0:T(1,128)} %bitcast.9, s32[1,128]{1,0:T(1,128)} %bitcast.11, ...), custom_call_target="tpu_custom_call" | custom-call | tf_op jit(solution)/shard_map/exchange/pallas_call | solution.py:348
  39.6 0.0 copy-done
  39.6 0.0 copy-done.1
  39.6 2.6 %conditional.1 = (bf16[128,2,4096]{2,1,0:T(2,128)(2,1)}, f32[128]{0:T(128)}) conditional(s32[]{:T(128)} %bitcast.6, (s32[8,128]{1,0:T(8,128)S(1)}, f32[1,128]{1,0:T(1,128)S(1)}, bf16[129,2,4096]{2,1,0:T(2,128)(2,1)S(1)}) %tuple.17, (s32[8,128]{1,0:T(8,128)S(1)}, bf16[129,2,4096]{2,1,0:T(2,128)(2,1)S(1)}, bf16[128,2,4096]{2,1,0:T(2,128)(2,1)}, ...), branch_computations={%region_0.0_spmd, %region_1.0_spmd} | conditional | flops 2097152 | bytes 12583952 | solution.py:391
  39.6 2.4 %arrange.2 = (bf16[128,2,4096]{2,1,0:T(2,128)(2,1)}, f32[1,128]{1,0:T(1,128)}) custom-call(s32[8,128]{1,0:T(8,128)S(1)} %get-tuple-element.25.table, f32[1,128]{1,0:T(1,128)S(1)} %get-tuple-element.26.adv_in, bf16[129,2,4096]{2,1,0:T(2,128)(2,1)S(1)} %get-tuple-element.27.rows_in), custom_call_target="tpu_custom_call" | custom-call | tf_op jit(solution)/shard_map/cond/branch_0_fun/arrange/pallas_call | solution.py:365
Async XLA Ops:
  0.6 39.0 %copy-start = (f32[4096]{0:T(1024)S(1)}, f32[4096]{0:T(1024)}, u32[]{:S(2)}) copy-start(f32[4096]{0:T(1024)} %param.8) | copy-start | bytes 49156
  0.6 39.0 %copy-start.1 = (s32[128]{0:T(128)S(1)}, s32[128]{0:T(128)}, u32[]{:S(2)}) copy-start(s32[128]{0:T(128)} %param.9) | copy-start | bytes 1540

commit v5 on v4

--- a/solution.py
+++ b/solution.py
@@ -1,7 +1,8 @@
-import functools
+import random
 
 import jax
 import jax.numpy as jnp
+import numpy as np
 from jax import lax
 from jax.experimental import pallas as pl
 from jax.experimental.pallas import tpu as pltpu
@@ -19,11 +20,24 @@
 READY = 16
 BATCH = 8
 LATE = 15
-STRIDE = 37
+SEED = 0
 norm_eps = 1e-05
 
 NT = (((1,), (1,)), ((), ()))
 NN = (((1,), (0,)), ((), ()))
+
+
+def hops(o):
+    return sum(min(k, 4 - k) for k in (o // 32, o // 8 % 4, o // 2 % 4))
+
+
+def make_order(seed):
+    rest = list(range(1, N))
+    random.Random(seed).shuffle(rest)
+    return [0] + sorted(rest, key=lambda o: hops(o) < 3)
+
+
+ORDER = make_order(SEED)
 
 
 def dot(a, b, dims, exact=False):
@@ -32,11 +46,6 @@
                                preferred_element_type=jnp.float32)
     return lax.dot_general(a.astype(jnp.bfloat16), b.astype(jnp.bfloat16), dims,
                            preferred_element_type=jnp.float32)
-
-
-def hops(i):
-    o = (i * STRIDE) % N
-    return sum(min(k, 4 - k) for k in (o // 32, o // 8 % 4, o // 2 % 4))
 
 
 class Place:
@@ -52,22 +61,16 @@
         self.xy = [[a + b for b in self.ys] for a in self.xs]
 
     def target(self, i):
-        o = (i * STRIDE) % N
+        o = ORDER[i]
         return self.xy[o // 32][o // 8 % 4] + self.zc[o // 2 % 4][o % 2]
 
-    def target_of(self, i):
-        o = lax.rem(i * STRIDE, N)
-        return (lax.rem(self.x + o // 32, 4) * 32 + lax.rem(self.y + lax.rem(o // 8, 4), 4) * 8
-                + lax.rem(self.z + lax.rem(o // 2, 4), 4) * 2 + lax.rem(self.core + lax.rem(o, 2), 2))
-
-    def all(self, i, sign):
-        o = (i * STRIDE) & (N - 1)
+    def all(self, o, sign):
         return ((((self.x + sign * (o >> 5)) & 3) << 5) + (((self.y + sign * ((o >> 3) & 3)) & 3) << 3)
                 + (((self.z + sign * ((o >> 1) & 3)) & 3) << 1) + ((self.core + o) & 1))
 
     def greet(self):
         barrier = pltpu.get_barrier_semaphore()
-        for i in sorted(range(1, N), key=hops, reverse=True):
+        for i in sorted(range(1, N), key=lambda i: -hops(ORDER[i])):
             pl.semaphore_signal(barrier, inc=1, device_id=self.target(i), device_id_type=LOGICAL)
         return barrier
 
@@ -105,13 +108,14 @@
                                         device_id=to, device_id_type=LOGICAL)
 
 
-def exchange(hidden, gain, prompt_of, lengths, reward, rows_out, table_out, flag_out, adv_out, weights_out,
-             hbuf, gbuf, tab, itab, stab, jtab, ttab, meta, meta_in, extra, piece_in, part, part_in, extra_in,
+def exchange(hidden, gain, prompt_of, lengths, reward, order, rows_out, table_out, flag_out, adv_out, weights_out,
+             hbuf, gbuf, obuf, tab, itab, stab, jtab, ttab, meta, meta_in, extra, piece_in, part, part_in, extra_in,
              send, recv, wtab, wsm, flag,
              in_sem, tab_sem, meta_send, meta_recv, piece_send, piece_recv, part_send, part_recv,
              send_sem, recv_sem):
     fetch_tab = [pltpu.make_async_copy(ref, tab.at[pl.ds(k, 1)], in_sem.at[2 + k])
                  for k, ref in enumerate((prompt_of, lengths, reward))]
+    fetch_tab.append(pltpu.make_async_copy(order, obuf, in_sem.at[5]))
     fetch_rows = pltpu.make_async_copy(hidden, hbuf, in_sem.at[0])
     fetch_gain = pltpu.make_async_copy(gain, gbuf, in_sem.at[1])
     for copy in fetch_tab:
@@ -128,7 +132,8 @@
     row8, lane8 = ints((8, N), 0), ints((8, N), 1)
     lane1 = ints((1, N), 1)
     lanef = lane8.astype(jnp.float32)
-    target = place.all(rows, 1)
+    by_sublane, by_lane = obuf[0:N], obuf[N:N + 8]
+    target = place.all(by_sublane, 1)
 
     prompt, length, level = tab[0:1], tab[1:2], tab[2:3]
     owner, label = prompt // OWN, lax.rem(prompt, OWN) + 1
@@ -194,15 +199,15 @@
     told_in = meta_in[...].astype(jnp.float32)
     by_step = dot(jnp.where(row8 == lane8, 1.0, 0.0), told_in, NT)
     label0, label1, to1, spares = by_step[0:1], by_step[3:4], by_step[6:7], by_step[7:8]
-    source = place.all(lane1, -1)
+    source = place.all(by_lane[0:1], -1)
 
     goes = to1 == target.astype(jnp.float32)
-    jtab[...] = dot(place.all(lane8, -1).astype(jnp.float32), jnp.where(goes, 1.0, 0.0), NT).astype(jnp.int32)
+    jtab[...] = dot(place.all(by_lane, -1).astype(jnp.float32), jnp.where(goes, 1.0, 0.0), NT).astype(jnp.int32)
     to_scalar = pltpu.make_async_copy(jtab, ttab, tab_sem.at[0])
     to_scalar.start()
     here = jnp.where(to1 == me.astype(jnp.float32), 1.0, 0.0)
 
-    ahead = jnp.where(place.all(rows, -1) < source, 1.0, 0.0)
+    ahead = jnp.where(place.all(by_sublane, -1) < source, 1.0, 0.0)
     group = (rows // G + 1).astype(jnp.float32)
     rank = lax.rem(rows, G).astype(jnp.float32)
     in0, in1 = jnp.where(label0 == group, 1.0, 0.0), jnp.where(label1 == group, 1.0, 0.0)
@@ -216,7 +221,7 @@
     facts1 = jnp.where(row8 == 0, by_step[4:5], jnp.where(row8 == 1, by_step[5:6], jnp.where(row8 == 2, 1.0 * N, lanef + N)))
     facts = dot(facts0, take0, NT) + dot(facts1, take1, NT)
 
-    flag[...] = worst.astype(jnp.int32)
+    flag[...] = jnp.where(worst > 1.5, 1, 0)
     flag_copy = pltpu.make_async_copy(flag, flag_out, in_sem.at[0])
     flag_copy.start()
     to_scalar.wait()
@@ -286,10 +291,10 @@
         whole(piece_in.at[pl.ds(0, PIECES)], piece_send).wait()
 
 
-def second(hidden, gain, prompt_of, weights, rows_out, hbuf, gbuf, tab, itab, stab, send, recv, wsm, outv,
-           in_sem, tab_sem, send_sem, recv_sem, out_sem):
+def second(hidden, gain, prompt_of, weights, order, rows_out, hbuf, gbuf, obuf, tab, itab, stab, send, recv, wsm,
+           in_sem, tab_sem, send_sem, recv_sem):
     copies = [pltpu.make_async_copy(a, b, in_sem.at[k]) for k, (a, b) in enumerate(
-        ((hidden, hbuf), (gain, gbuf), (prompt_of, tab.at[pl.ds(0, 1)]), (weights, wsm)))]
+        ((hidden, hbuf), (gain, gbuf), (prompt_of, tab.at[pl.ds(0, 1)]), (weights, wsm), (order, obuf)))]
     for copy in copies:
         copy.start()
     place = Place()
@@ -297,7 +302,7 @@
     for copy in copies:
         copy.wait()
     rows, lanes = ints((N, N), 0), ints((N, N), 1)
-    slot1 = split(tab[0:1] // OWN, place.all(rows, 1), jnp.where(rows < lanes, 1.0, 0.0))[1]
+    slot1 = split(tab[0:1] // OWN, place.all(obuf[0:N], 1), jnp.where(rows < lanes, 1.0, 0.0))[1]
     itab[...] = dot(ints((8, N), 1).astype(jnp.float32), slot1, NT).astype(jnp.int32)
     to_scalar = pltpu.make_async_copy(itab, stab, tab_sem)
     to_scalar.start()
@@ -310,28 +315,45 @@
     lax.fori_loop(0, N, pack, 0)
     pltpu.make_async_copy(send.at[0], recv.at[0], recv_sem).start()
 
-    def ship(i, _):
-        remote(send.at[i], recv.at[i], send_sem, recv_sem, place.target_of(i)).start()
-        return 0
-    lax.fori_loop(1, N, ship, 0)
+    for i in range(1, N):
+        remote(send.at[i], recv.at[i], send_sem, recv_sem, place.target(i)).start()
     whole(recv, recv_sem).wait()
     gains = gbuf[...]
 
     def settle(i, _):
-        outv[i] = weighed(normed(recv[i], gains), wsm[0, i], wsm[1, i])
+        rows_out[i] = weighed(normed(recv[i], gains), wsm[0, i], wsm[1, i])
         return 0
     lax.fori_loop(0, N, settle, 0)
     whole(send.at[pl.ds(0, N - 1)], send_sem).wait()
-    put = pltpu.make_async_copy(outv, rows_out, out_sem)
-    put.start()
-    put.wait()
-
-
-def arrange(table, adv_in, rows_in, out, adv_out, sem):
+
+
+def arrange(table, adv_in, rows_in, out, adv_out, sem, adv_sem):
+    put_adv = pltpu.make_async_copy(adv_in, adv_out, adv_sem)
+    put_adv.start()
     for q in range(N):
-        pltpu.make_async_copy(rows_in.at[bounded(table[0, q], rows_in.shape[0])], out.at[q], sem).start()
-    adv_out[...] = adv_in[...]
+        pltpu.make_async_copy(rows_in.at[bounded(table[0, q], N + 1)], out.at[q], sem).start()
     whole(out, sem).wait()
+    put_adv.wait()
+
+
+def arrange_both(table, adv_in, rows_in, more_in, out, adv_out, sem, adv_sem):
+    put_adv = pltpu.make_async_copy(adv_in, adv_out, adv_sem)
+    put_adv.start()
+
+    def put(q, _):
+        i = bounded(table[1, q], 2 * N)
+
+        @pl.when(i < N)
+        def _():
+            pltpu.make_async_copy(rows_in.at[i], out.at[q], sem).start()
+
+        @pl.when(i >= N)
+        def _():
+            pltpu.make_async_copy(more_in.at[i - N], out.at[q], sem).start()
+        return 0
+    lax.fori_loop(0, N, put, 0)
+    whole(out, sem).wait()
+    put_adv.wait()
 
 
 def on_device(hidden, norm_gain, prompt_of, lengths, reward_level):
@@ -344,51 +366,53 @@
     block = pltpu.VMEM((N, window, features), bf16)
     square, strip = pltpu.VMEM((N, N), i32), pltpu.VMEM((8, N), i32)
     gains = pltpu.VMEM((1, features), f32)
+    steps = pltpu.VMEM((N + 8, N), i32)
+    order = jnp.asarray(np.concatenate([np.repeat(np.array(ORDER, np.int32)[:, None], N, 1), np.repeat(np.array([ORDER], np.int32), 8, 0)]))
     gain, prompt, length, level = (a.reshape(1, a.shape[0]) for a in (norm_gain, prompt_of, lengths, reward_level))
     rows, table, flag, adv, weights = pl.pallas_call(
         exchange,
         out_shape=(shape((N + 1, window, features), bf16), shape((8, N), i32), shape((1, 1), i32),
                    shape((1, N), f32), shape((8, N), f32)),
-        in_specs=[any_space] * 5,
+        in_specs=[any_space] * 6,
         out_specs=(vmem, vmem, any_space, vmem, vmem),
         scratch_shapes=[
-            block, gains, strip, strip, pltpu.SMEM((8, N), i32), strip, pltpu.SMEM((8, N), i32), square, square,
+            block, gains, steps, strip, strip, pltpu.SMEM((8, N), i32), strip, pltpu.SMEM((8, N), i32), square, square,
             pltpu.VMEM((window, features), bf16), pltpu.VMEM((N, window, 128), bf16),
             pltpu.VMEM((N, window, 128), bf16), pltpu.VMEM((PIECES, window, 128), bf16), pltpu.VMEM((window, features), bf16),
             block, block, pltpu.VMEM((2, 8, N), f32), pltpu.SMEM((2, 8, N), f32), pltpu.VMEM((1, 1), i32),
-            dma((5,)), dma((2,)), dma, dma, dma, dma, dma, dma, dma, dma((N // BATCH,))],
+            dma((6,)), dma((2,)), dma, dma, dma, dma, dma, dma, dma, dma((N // BATCH,))],
         compiler_params=pltpu.CompilerParams(collective_id=0, has_side_effects=True),
         name="exchange",
-    )(hidden, gain, prompt, length, level)
-
-    def put(table, adv, rows):
+    )(hidden, gain, prompt, length, level, order)
+
+    def put(kernel, *row_blocks):
         return pl.pallas_call(
-            arrange,
+            kernel,
             out_shape=(shape((N, window, features), bf16), shape((1, N), f32)),
-            in_specs=[pl.BlockSpec(memory_space=pltpu.SMEM), vmem, any_space],
-            out_specs=(any_space, vmem),
-            scratch_shapes=[dma],
-            name="arrange",
-        )(table, adv, rows)
+            in_specs=[pl.BlockSpec(memory_space=pltpu.SMEM)] + [any_space] * (1 + len(row_blocks)),
+            out_specs=(any_space, any_space),
+            scratch_shapes=[dma, dma],
+            name=kernel.__name__,
+        )(table, adv, *row_blocks)
 
     def few(_):
-        return put(table, adv, rows)
+        return put(arrange, rows)
 
     def many(_):
         more = pl.pallas_call(
             second,
             out_shape=shape((N, window, features), bf16),
-            in_specs=[any_space] * 4,
-            out_specs=any_space,
+            in_specs=[any_space] * 5,
+            out_specs=vmem,
             scratch_shapes=[
-                block, gains, strip, strip, pltpu.SMEM((8, N), i32), block, block, pltpu.SMEM((8, N), f32), block,
-                dma((4,)), dma, dma, dma, dma],
-            compiler_params=pltpu.CompilerParams(collective_id=1, has_side_effects=True),
+                block, gains, steps, strip, strip, pltpu.SMEM((8, N), i32), block, block, pltpu.SMEM((8, N), f32),
+                dma((5,)), dma, dma, dma],
+            compiler_params=pltpu.CompilerParams(collective_id=1, has_side_effects=True, vmem_limit_bytes=24 << 20),
             name="second",
-        )(hidden, gain, prompt, weights)
-        return put(table[1:2], adv, jnp.concatenate([rows[:N], more]))
-
-    out, adv = lax.cond(flag[0, 0] > 1, many, few, 0)
+        )(hidden, gain, prompt, weights, order)
+        return put(arrange_both, rows, more)
+
+    out, adv = lax.switch(flag[0, 0], (few, many), 0)
     return out, adv.reshape(N)
 
 

time: 42.5 us -> 41.7 us (0.981)
  Pallas kernels: 40.7 us -> 40.2 us
    pallas_call x1, Pallas kernels: 2.4 us -> 1.9 us  [put(): pl.pallas_call(kernel, out_shape=(shape((N, window, features), bf16), sha...]
where the time goes in v5:
time: 41.7 us; the launch traced here: 41.6 us
  Pallas kernels  40.2 us (96%)
  between operations  1.37 us (3%)
    pallas_call x1, Pallas kernels, on_device(): pl.pallas_call(exchange, out_shape=(shape((N + 1, window, features), bf16...  38.3 us
    pallas_call x1, Pallas kernels, put(): pl.pallas_call(kernel, out_shape=(shape((N, window, features), bf16), sha...  1.9 us

profile of v5, /device:TPU:1, one launch (start us, length us, event | category | flops | bytes accessed | tf_op | source)
XLA Modules:
  0.0 41.6 jit_solution(13459717224148445839)
XLA Ops:
  0.6 0.0 copy-start.1
  0.6 0.0 copy-start.3
  0.7 0.0 copy-start.2
  0.7 38.3 %exchange.1 = (bf16[129,2,4096]{2,1,0:T(2,128)(2,1)S(1)}, s32[8,128]{1,0:T(8,128)S(1)}, s32[1,1]{1,0:T(1,128)}, f32[1,128]{1,0:T(1,128)S(1)}, f32[8,128]{1,0:T(8,128)S(1)}) custom-call(bf16[128,2,4096]{2,1,0:T(2,128)(2,1)} %hidden.1, f32[1,4096]{1,0:T(1,128)} %bitcast.7, s32[1,128]{1,0:T(1,128)} %bitcast.9, s32[1,128]{1,0:T(1,128)} %bitcast.11, ...), custom_call_target="tpu_custom_call" | custom-call | tf_op jit(solution)/shard_map/exchange/pallas_call | solution.py:372
  39.6 0.0 copy-done.1
  39.7 0.0 copy-done.3
  39.7 0.0 copy-done.2
  39.7 1.9 %conditional.1 = (bf16[128,2,4096]{2,1,0:T(2,128)(2,1)}, f32[128]{0:T(128)}) conditional(s32[]{:T(128)} %bitcast.6, (s32[8,128]{1,0:T(8,128)S(1)}, f32[1,128]{1,0:T(1,128)S(1)}, bf16[129,2,4096]{2,1,0:T(2,128)(2,1)S(1)}) %tuple.17, (bf16[128,2,4096]{2,1,0:T(2,128)(2,1)}, f32[1,4096]{1,0:T(1,128)S(1)}, s32[1,128]{1,0:T(1,128)S(1)}, ...), branch_computations={%region_0.0_spmd, %region_1.0_spmd} | conditional | bytes 8388652 | solution.py:415
  39.7 1.9 %arrange.1 = (bf16[128,2,4096]{2,1,0:T(2,128)(2,1)}, f32[1,128]{1,0:T(1,128)}) custom-call(s32[8,128]{1,0:T(8,128)S(1)} %get-tuple-element.27.table, f32[1,128]{1,0:T(1,128)S(1)} %get-tuple-element.28.adv_in, bf16[129,2,4096]{2,1,0:T(2,128)(2,1)S(1)} %get-tuple-element.29.rows_in), custom_call_target="tpu_custom_call" | custom-call | tf_op jit(solution)/shard_map/cond/branch_0_fun/arrange/pallas_call | solution.py:389
Async XLA Ops:
  0.6 39.0 %copy-start.1 = (s32[136,128]{1,0:T(8,128)S(1)}, s32[136,128]{1,0:T(8,128)}, u32[]{:S(2)}) copy-start(s32[136,128]{1,0:T(8,128)} %constant.8.clone.order) | copy-start | bytes 208900
  0.6 39.0 %copy-start.3 = (s32[128]{0:T(128)S(1)}, s32[128]{0:T(128)}, u32[]{:S(2)}) copy-start(s32[128]{0:T(128)} %param.10) | copy-start | bytes 1540
  0.7 39.0 %copy-start.2 = (f32[4096]{0:T(1024)S(1)}, f32[4096]{0:T(1024)}, u32[]{:S(2)}) copy-start(f32[4096]{0:T(1024)} %param.9) | copy-start | bytes 49156

commit v6 on v5

--- a/solution.py
+++ b/solution.py
@@ -1,3 +1,4 @@
+import functools
 import random
 
 import jax
@@ -14,10 +15,9 @@
 G = 16
 OWN = 8
 PIECES = 32
-EARLY = 48
+RAW = 80
+EARLY = 80
 LEAD = 4
-FIRST = 8
-READY = 16
 BATCH = 8
 LATE = 15
 SEED = 0
@@ -109,9 +109,9 @@
 
 
 def exchange(hidden, gain, prompt_of, lengths, reward, order, rows_out, table_out, flag_out, adv_out, weights_out,
-             hbuf, gbuf, obuf, tab, itab, stab, jtab, ttab, meta, meta_in, extra, piece_in, part, part_in, extra_in,
+             hbuf, gbuf, obuf, tab, itab, stab, jtab, ttab, meta, meta_in, share, share_in, extra, piece_in, part, part_in, extra_in,
              send, recv, wtab, wsm, flag,
-             in_sem, tab_sem, meta_send, meta_recv, piece_send, piece_recv, part_send, part_recv,
+             in_sem, tab_sem, meta_send, meta_recv, share_send, share_recv, piece_send, piece_recv, part_send, part_recv,
              send_sem, recv_sem):
     fetch_tab = [pltpu.make_async_copy(ref, tab.at[pl.ds(k, 1)], in_sem.at[2 + k])
                  for k, ref in enumerate((prompt_of, lengths, reward))]
@@ -137,19 +137,24 @@
 
     prompt, length, level = tab[0:1], tab[1:2], tab[2:3]
     owner, label = prompt // OWN, lax.rem(prompt, OWN) + 1
-    slot0, slot1 = split(owner, target, jnp.where(rows < lanes, 1.0, 0.0))
-    twice = jnp.sum(slot1, axis=0, keepdims=True)
+    slot0, slot1 = split(owner, rows, jnp.where(rows < lanes, 1.0, 0.0))
+    once, twice = jnp.sum(slot0, axis=0, keepdims=True), jnp.sum(slot1, axis=0, keepdims=True)
     spare = jnp.sum(twice, axis=1, keepdims=True)
     spare_row = jnp.sum(twice * lane1.astype(jnp.float32), axis=1, keepdims=True)
     spare_to = jnp.where(spare > 0.5, jnp.sum(twice * owner.astype(jnp.float32), axis=1, keepdims=True), -1.0)
     itab[...] = jnp.where(row8 == 0, dot(lanef, slot0, NT), spare_row).astype(jnp.int32)
     to_scalar = pltpu.make_async_copy(itab, stab, tab_sem.at[0])
     to_scalar.start()
+
+    number, member = rows & 7, (rows >> 3) == (owner & 3)
     zero = jnp.zeros((N, N), jnp.int32)
-    told = jnp.where(rows == 0, label, jnp.where(rows == 1, level, jnp.where(rows == 2, length, zero)))
-    told1 = jnp.where(rows == 3, label, jnp.where(rows == 4, level, jnp.where(rows == 5, length, zero)))
-    meta[...] = (dot(slot0, told.astype(jnp.float32), NT) + dot(slot1, told1.astype(jnp.float32), NT)
-                 + jnp.where(lanes == 6, spare_to, jnp.where(lanes == 7, spare, 0.0))).astype(jnp.int32)
+    told0 = jnp.where(number == 0, label, jnp.where(number == 1, level, jnp.where(number == 2, length, zero)))
+    told1 = jnp.where(number == 3, label, jnp.where(number == 4, level, jnp.where(number == 5, length, zero)))
+    told0, told1 = (jnp.where(member, told, zero).astype(jnp.float32) for told in (told0, told1))
+    cell = jnp.where((owner >> 2) == ints((PIECES, N), 0), 1.0, 0.0)
+    lane32 = ints((PIECES, N), 1)
+    meta[...] = (dot(cell * once, told0, NT) + dot(cell * twice, told1, NT)
+                 + jnp.where(lane32 == 32, spare_to, jnp.where(lane32 == 33, spare, 0.0))).astype(jnp.int32)
     to_scalar.wait()
     fetch_gain.wait()
     gains = gbuf[...]
@@ -158,53 +163,77 @@
 
     def pack(i):
         if i < N:
-            send[i] = normed(hbuf[bounded(stab[0, i], N)], gains)
+            row = hbuf[bounded(stab[0, place.target(i)], N)]
+            send[i] = row if i < RAW else normed(row, gains)
 
     def ship(i):
         remote(send.at[i], recv.at[i], send_sem, recv_sem.at[i // BATCH], place.target(i)).start()
 
-    def hand(r):
+    def hand(r, copy):
         t = lax.rem(me // 4 + r, PIECES)
-        return extra.at[:, pl.ds(pl.multiple_of(t * 128, 128), 128)], 4 * t
+        copy(meta.at[pl.ds(t, 1)], meta_in.at[pl.ds(me, 1)], meta_send, meta_recv, 4 * t)
+        copy(extra.at[:, pl.ds(pl.multiple_of(t * 128, 128), 128)], piece_in.at[me], piece_send, piece_recv, 4 * t)
+
+    def away(src, dst, send_sem, recv_sem, to):
+        remote(src, dst, send_sem, recv_sem, to).start()
+
+    def at_home(src, dst, send_sem, recv_sem, to):
+        pltpu.make_async_copy(src, dst, recv_sem).start()
 
     relay = lax.rem(me, 4) == 0
-    for i in range(READY):
+    for i in range(RAW):
         pack(i)
     pltpu.make_async_copy(send.at[0], recv.at[0], recv_sem.at[0]).start()
-    pltpu.make_async_copy(meta.at[pl.ds(0, 1)], meta_in.at[pl.ds(0, 1)], meta_recv).start()
 
     @pl.when(relay)
     def _():
-        pltpu.make_async_copy(hand(0)[0], piece_in.at[me], piece_recv).start()
+        hand(0, at_home)
 
     pl.semaphore_wait(barrier, N - 1)
-
-    for i in range(1, FIRST):
-        ship(i)
-    for i in range(1, N):
-        remote(meta.at[pl.ds(i, 1)], meta_in.at[pl.ds(i, 1)], meta_send, meta_recv, place.target(i)).start()
 
     @pl.when(jnp.logical_not(relay))
     def _():
-        tile, to = hand(0)
-        remote(tile, piece_in.at[me], piece_send, piece_recv, to).start()
+        hand(0, away)
     for r in range(1, PIECES):
-        tile, to = hand(r)
-        remote(tile, piece_in.at[me], piece_send, piece_recv, to).start()
-    for i in range(FIRST, EARLY):
-        pack(i - FIRST + READY)
+        hand(r, away)
+    for i in range(1, RAW):
         ship(i)
-
-    whole(meta_in, meta_recv).wait()
-    told_in = meta_in[...].astype(jnp.float32)
-    by_step = dot(jnp.where(row8 == lane8, 1.0, 0.0), told_in, NT)
+    for i in range(RAW, EARLY + LEAD):
+        pack(i)
+        if i >= RAW + LEAD:
+            ship(i - LEAD)
+
+    @pl.when(relay)
+    def _():
+        whole(meta_in, meta_recv).wait()
+        told_in = meta_in[...].astype(jnp.float32)
+        for u in range(4):
+            wanted = jnp.where(row8 < 6, row8 + 8 * u, row8 + 26)
+            share[u] = dot(jnp.where(lane8 == wanted, 1.0, 0.0), told_in, NT).astype(jnp.int32)
+        goes = share[0, 6:7, :] == target
+        jtab[...] = dot(lanef, jnp.where(goes, 1.0, 0.0), NT).astype(jnp.int32)
+        to_scalar = pltpu.make_async_copy(jtab, ttab, tab_sem.at[0])
+        to_scalar.start()
+        to_scalar.wait()
+        pltpu.make_async_copy(share.at[0], share_in, share_recv).start()
+        for u in range(1, 4):
+            remote(share.at[u], share_in, share_send, share_recv, me + u).start()
+        whole(piece_in, piece_recv).wait()
+        for i in range(N):
+            part[i] = piece_in[bounded(ttab[0, i], N)]
+        pltpu.make_async_copy(part.at[0], part_in.at[me // 4], part_recv).start()
+        for i in range(1, N):
+            remote(part.at[i], part_in.at[me // 4], part_send, part_recv, place.target(i)).start()
+
+    for i in range(EARLY, N):
+        pack(i + LEAD)
+        ship(i)
+
+    whole(share_in, share_recv).wait()
+    source = place.all(by_lane[0:1], -1)
+    by_step = dot(share_in[...].astype(jnp.float32), jnp.where(rows == source, 1.0, 0.0), NN)
     label0, label1, to1, spares = by_step[0:1], by_step[3:4], by_step[6:7], by_step[7:8]
-    source = place.all(by_lane[0:1], -1)
-
-    goes = to1 == target.astype(jnp.float32)
-    jtab[...] = dot(place.all(by_lane, -1).astype(jnp.float32), jnp.where(goes, 1.0, 0.0), NT).astype(jnp.int32)
-    to_scalar = pltpu.make_async_copy(jtab, ttab, tab_sem.at[0])
-    to_scalar.start()
+    goes = to1 == rows.astype(jnp.float32)
     here = jnp.where(to1 == me.astype(jnp.float32), 1.0, 0.0)
 
     ahead = jnp.where(place.all(by_sublane, -1) < source, 1.0, 0.0)
@@ -224,27 +253,6 @@
     flag[...] = jnp.where(worst > 1.5, 1, 0)
     flag_copy = pltpu.make_async_copy(flag, flag_out, in_sem.at[0])
     flag_copy.start()
-    to_scalar.wait()
-
-    @pl.when(relay)
-    def _():
-        whole(piece_in, piece_recv).wait()
-        for i in range(N):
-            part[i] = piece_in[bounded(ttab[0, i], N)]
-        for i in range(EARLY, EARLY + LEAD):
-            ship(i)
-        pltpu.make_async_copy(part.at[0], part_in.at[me // 4], part_recv).start()
-        for i in range(1, N):
-            remote(part.at[i], part_in.at[me // 4], part_send, part_recv, place.target(i)).start()
-
-    @pl.when(jnp.logical_not(relay))
-    def _():
-        for i in range(EARLY, EARLY + LEAD):
-            ship(i)
-    for i in range(EARLY + LEAD, N):
-        pack(i - FIRST - LEAD + READY)
-        ship(i)
-
     same = jnp.where(rows // G == lanes // G, 1.0, 0.0)
     mean = dot(facts, same, NN) * (1.0 / G)
     centred = facts - mean
@@ -263,31 +271,35 @@
     adv_out[...] = adv
     to_scalar.wait()
 
-    def settle(g, _):
+    def settle(raw, g, _):
         whole(recv.at[pl.ds(0, BATCH)], recv_sem.at[g]).wait()
         for k in range(BATCH):
             i = g * BATCH + k
-            rows_out[i] = weighed(recv[i], wsm[0, 0, i], wsm[0, 1, i])
+            row = normed(recv[i], gains) if raw else recv[i]
+            rows_out[i] = weighed(row, wsm[0, 0, i], wsm[0, 1, i])
         return 0
-    lax.fori_loop(0, LATE, settle, 0)
+    lax.fori_loop(0, RAW // BATCH, functools.partial(settle, True), 0)
+    lax.fori_loop(RAW // BATCH, LATE, functools.partial(settle, False), 0)
 
     whole(part_in, part_recv).wait()
     for t in range(PIECES):
         extra_in[:, pl.ds(t * 128, 128)] = part_in[t]
     rows_out[N] = weighed(extra_in[...], wsm[1, 0, 0], wsm[1, 1, 0])
-    lax.fori_loop(LATE, N // BATCH, settle, 0)
-
-    whole(meta.at[pl.ds(0, N - 1)], meta_send).wait()
+    lax.fori_loop(LATE, N // BATCH, functools.partial(settle, False), 0)
+
     whole(send.at[pl.ds(0, N - 1)], send_sem).wait()
     flag_copy.wait()
 
     @pl.when(relay)
     def _():
+        whole(meta.at[pl.ds(0, PIECES - 1)], meta_send).wait()
         whole(piece_in.at[pl.ds(0, PIECES - 1)], piece_send).wait()
+        whole(share.at[pl.ds(0, 3)], share_send).wait()
         whole(part.at[pl.ds(0, N - 1)], part_send).wait()
 
     @pl.when(jnp.logical_not(relay))
     def _():
+        whole(meta, meta_send).wait()
         whole(piece_in.at[pl.ds(0, PIECES)], piece_send).wait()
 
 
@@ -376,11 +388,12 @@
         in_specs=[any_space] * 6,
         out_specs=(vmem, vmem, any_space, vmem, vmem),
         scratch_shapes=[
-            block, gains, steps, strip, strip, pltpu.SMEM((8, N), i32), strip, pltpu.SMEM((8, N), i32), square, square,
+            block, gains, steps, strip, strip, pltpu.SMEM((8, N), i32), strip, pltpu.SMEM((8, N), i32),
+            pltpu.VMEM((PIECES, N), i32), square, pltpu.VMEM((4, 8, N), i32), strip,
             pltpu.VMEM((window, features), bf16), pltpu.VMEM((N, window, 128), bf16),
             pltpu.VMEM((N, window, 128), bf16), pltpu.VMEM((PIECES, window, 128), bf16), pltpu.VMEM((window, features), bf16),
             block, block, pltpu.VMEM((2, 8, N), f32), pltpu.SMEM((2, 8, N), f32), pltpu.VMEM((1, 1), i32),
-            dma((6,)), dma((2,)), dma, dma, dma, dma, dma, dma, dma, dma((N // BATCH,))],
+            dma((6,)), dma((2,)), dma, dma, dma, dma, dma, dma, dma, dma, dma, dma((N // BATCH,))],
         compiler_params=pltpu.CompilerParams(collective_id=0, has_side_effects=True),
         name="exchange",
     )(hidden, gain, prompt, length, level, order)

time: 41.7 us -> 40.6 us (0.974)
  Pallas kernels: 40.2 us -> 39 us
    pallas_call x1, Pallas kernels: 38.3 us -> 37.1 us  [on_device(): pl.pallas_call(exchange, out_shape=(shape((N + 1, window, features), bf16...]
where the time goes in v6:
time: 40.6 us; the launch traced here: 40.4 us
  Pallas kernels  39 us (96%)
  between operations  1.37 us (3%)
    pallas_call x1, Pallas kernels, on_device(): pl.pallas_call(exchange, out_shape=(shape((N + 1, window, features), bf16...  37.1 us
    pallas_call x1, Pallas kernels, put(): pl.pallas_call(kernel, out_shape=(shape((N, window, features), bf16), sha...  1.9 us

profile of v6, /device:TPU:1, one launch (start us, length us, event | category | flops | bytes accessed | tf_op | source)
XLA Modules:
  0.0 40.4 jit_solution(17532934759620659117)
XLA Ops:
  0.6 0.0 copy-start.1
  0.6 0.0 copy-start.3
  0.7 0.0 copy-start.2
  0.7 37.1 %exchange.1 = (bf16[129,2,4096]{2,1,0:T(2,128)(2,1)S(1)}, s32[8,128]{1,0:T(8,128)S(1)}, s32[1,1]{1,0:T(1,128)}, f32[1,128]{1,0:T(1,128)S(1)}, f32[8,128]{1,0:T(8,128)S(1)}) custom-call(bf16[128,2,4096]{2,1,0:T(2,128)(2,1)} %hidden.1, f32[1,4096]{1,0:T(1,128)} %bitcast.7, s32[1,128]{1,0:T(1,128)} %bitcast.9, s32[1,128]{1,0:T(1,128)} %bitcast.11, ...), custom_call_target="tpu_custom_call" | custom-call | tf_op jit(solution)/shard_map/exchange/pallas_call | solution.py:384
  38.4 0.0 copy-done.1
  38.4 0.0 copy-done.3
  38.4 0.0 copy-done.2
  38.4 1.9 %conditional.1 = (bf16[128,2,4096]{2,1,0:T(2,128)(2,1)}, f32[128]{0:T(128)}) conditional(s32[]{:T(128)} %bitcast.6, (s32[8,128]{1,0:T(8,128)S(1)}, f32[1,128]{1,0:T(1,128)S(1)}, bf16[129,2,4096]{2,1,0:T(2,128)(2,1)S(1)}) %tuple.17, (bf16[128,2,4096]{2,1,0:T(2,128)(2,1)}, f32[1,4096]{1,0:T(1,128)S(1)}, s32[1,128]{1,0:T(1,128)S(1)}, ...), branch_computations={%region_0.0_spmd, %region_1.0_spmd} | conditional | bytes 8388652 | solution.py:428
  38.5 1.9 %arrange.1 = (bf16[128,2,4096]{2,1,0:T(2,128)(2,1)}, f32[1,128]{1,0:T(1,128)}) custom-call(s32[8,128]{1,0:T(8,128)S(1)} %get-tuple-element.27.table, f32[1,128]{1,0:T(1,128)S(1)} %get-tuple-element.28.adv_in, bf16[129,2,4096]{2,1,0:T(2,128)(2,1)S(1)} %get-tuple-element.29.rows_in), custom_call_target="tpu_custom_call" | custom-call | tf_op jit(solution)/shard_map/cond/branch_0_fun/arrange/pallas_call | solution.py:402
Async XLA Ops:
  0.6 37.8 %copy-start.1 = (s32[136,128]{1,0:T(8,128)S(1)}, s32[136,128]{1,0:T(8,128)}, u32[]{:S(2)}) copy-start(s32[136,128]{1,0:T(8,128)} %constant.8.clone.order) | copy-start | bytes 208900
  0.6 37.8 %copy-start.3 = (s32[128]{0:T(128)S(1)}, s32[128]{0:T(128)}, u32[]{:S(2)}) copy-start(s32[128]{0:T(128)} %param.10) | copy-start | bytes 1540
  0.7 37.8 %copy-start.2 = (f32[4096]{0:T(1024)S(1)}, f32[4096]{0:T(1024)}, u32[]{:S(2)}) copy-start(f32[4096]{0:T(1024)} %param.9) | copy-start | bytes 49156

commit v7 on v6

--- a/solution.py
+++ b/solution.py
@@ -18,8 +18,8 @@
 RAW = 80
 EARLY = 80
 LEAD = 4
-BATCH = 8
-LATE = 15
+BATCH = 16
+LATE = 7
 SEED = 0
 norm_eps = 1e-05
 

time: 40.6 us -> 40.5 us (level)
  no operation moved by 1% of the time
where the time goes in v7:
time: 40.5 us; the launch traced here: 40.4 us
  Pallas kernels  39 us (96%)
  between operations  1.37 us (3%)
    pallas_call x1, Pallas kernels, on_device(): pl.pallas_call(exchange, out_shape=(shape((N + 1, window, features), bf16...  37.1 us
    pallas_call x1, Pallas kernels, put(): pl.pallas_call(kernel, out_shape=(shape((N, window, features), bf16), sha...  1.9 us

profile of v7, /device:TPU:1, one launch (start us, length us, event | category | flops | bytes accessed | tf_op | source)
XLA Modules:
  0.0 40.4 jit_solution(16130665108111705067)
XLA Ops:
  0.6 0.0 copy-start.1
  0.6 0.0 copy-start.3
  0.7 0.0 copy-start.2
  0.7 37.1 %exchange.1 = (bf16[129,2,4096]{2,1,0:T(2,128)(2,1)S(1)}, s32[8,128]{1,0:T(8,128)S(1)}, s32[1,1]{1,0:T(1,128)}, f32[1,128]{1,0:T(1,128)S(1)}, f32[8,128]{1,0:T(8,128)S(1)}) custom-call(bf16[128,2,4096]{2,1,0:T(2,128)(2,1)} %hidden.1, f32[1,4096]{1,0:T(1,128)} %bitcast.7, s32[1,128]{1,0:T(1,128)} %bitcast.9, s32[1,128]{1,0:T(1,128)} %bitcast.11, ...), custom_call_target="tpu_custom_call" | custom-call | tf_op jit(solution)/shard_map/exchange/pallas_call | solution.py:384
  38.4 0.0 copy-done.1
  38.4 0.0 copy-done.3
  38.5 0.0 copy-done.2
  38.5 1.9 %conditional.1 = (bf16[128,2,4096]{2,1,0:T(2,128)(2,1)}, f32[128]{0:T(128)}) conditional(s32[]{:T(128)} %bitcast.6, (s32[8,128]{1,0:T(8,128)S(1)}, f32[1,128]{1,0:T(1,128)S(1)}, bf16[129,2,4096]{2,1,0:T(2,128)(2,1)S(1)}) %tuple.17, (bf16[128,2,4096]{2,1,0:T(2,128)(2,1)}, f32[1,4096]{1,0:T(1,128)S(1)}, s32[1,128]{1,0:T(1,128)S(1)}, ...), branch_computations={%region_0.0_spmd, %region_1.0_spmd} | conditional | bytes 8388652 | solution.py:428
  38.5 1.9 %arrange.1 = (bf16[128,2,4096]{2,1,0:T(2,128)(2,1)}, f32[1,128]{1,0:T(1,128)}) custom-call(s32[8,128]{1,0:T(8,128)S(1)} %get-tuple-element.27.table, f32[1,128]{1,0:T(1,128)S(1)} %get-tuple-element.28.adv_in, bf16[129,2,4096]{2,1,0:T(2,128)(2,1)S(1)} %get-tuple-element.29.rows_in), custom_call_target="tpu_custom_call" | custom-call | tf_op jit(solution)/shard_map/cond/branch_0_fun/arrange/pallas_call | solution.py:402
Async XLA Ops:
  0.6 37.8 %copy-start.1 = (s32[136,128]{1,0:T(8,128)S(1)}, s32[136,128]{1,0:T(8,128)}, u32[]{:S(2)}) copy-start(s32[136,128]{1,0:T(8,128)} %constant.8.clone.order) | copy-start | bytes 208900
  0.6 37.8 %copy-start.3 = (s32[128]{0:T(128)S(1)}, s32[128]{0:T(128)}, u32[]{:S(2)}) copy-start(s32[128]{0:T(128)} %param.10) | copy-start | bytes 1540
  0.7 37.8 %copy-start.2 = (f32[4096]{0:T(1024)S(1)}, f32[4096]{0:T(1024)}, u32[]{:S(2)}) copy-start(f32[4096]{0:T(1024)} %param.9) | copy-start | bytes 49156
